TPU v7x, 256 devices: a whole 4x4x8 slice. The times are simulated.
256 devices in a mesh: oct: 256 (over y, x, z, core).
Axes of the slice: x: 4, y: 4, z: 8, core: 2. Of those that a mesh axis runs over, the one named last changes fastest.
Arguments:
- leaf_spectra: bfloat16 [65536, 2016], P('oct'), may hold values from -6 to 6
- leaf_keys: int32 [65536], P('oct'), may hold values from 8 to 393223, as said below
- parent_keys: int32 [16384], P('oct'), may hold values from 1 to 49152, as said below
- child_phase: float32 [8, 1008], replicated, may hold values from -3.140625 to 3.140625
- coarsen: bfloat16 [2, 1008, 1008], replicated, may hold values from -0.0625 to 0.0625
- transfer: bfloat16 [316, 2016], replicated, may hold values from -0.3125 to 0.3125
- vlist_src: int32 [16384, 189], P('oct'), may hold values from -1 to 511, as said below
- vlist_type: int32 [16384, 189], P('oct'), may hold values from 0 to 315
Outputs:
- upward: bfloat16 [16384, 2016], P('oct')
- local_field: bfloat16 [16384, 2016], P('oct')
Inputs may be any that keep to these rules, and one draw needn't show every extreme that they name: leaf_keys: strictly increasing. Every leaf_keys // 8 is a value of parent_keys. The leaves of a parent lie on the device that owns it, except that some of the leaves of a device's last parent (at least one, at most two) are the first leaves of the next device; every device but the first begins so, and the last device's parents have all their leaves at home. parent_keys: strictly increasing; every parent has 1 to 8 leaves. `vlist_src`: in each row the live entries come first, then -1. A live entry is the index of a source parent within the target's window: the 512 parents that end with the last parent of the target's block of 64, counted cyclically. Every target has at least 94 live entries, and on every device some target has all 189 live.
All inputs are finite; a program needn't handle non-finite values.
Results may differ from a plain program's by a relative error of at most 0.0058.
Values may be sent and summed in bfloat16 or wider, within the bound.
No kernel may reach another device: no remote copies, remote signals or barrier semaphores. Data moves between devices by JAX's collectives and lax.ppermute only.
A program may use at most 64 MiB of HBM per device.

v0:
```python
import jax
import jax.numpy as jnp
from jax import lax
from jax.experimental import pallas as pl
from jax.experimental.pallas import tpu as pltpu
from jax.sharding import PartitionSpec as P


F32 = jnp.float32
BF16 = jnp.bfloat16
LANES = 128
HELD = 4
UNROLL = 16
ROW = 256
DEAD = 1 << 20


def lane_of(shape):
    return lax.broadcasted_iota(jnp.int32, shape, 1)


def split_halves(tile_of, half):
    count = -(-half // LANES)
    tail = half - (count - 1) * LANES
    shift = LANES - tail
    total = -(-2 * half // LANES)
    real, imag = [], []
    for k in range(count):
        tile = tile_of(k)
        if k == count - 1:
            tile = jnp.where(lane_of(tile.shape) < tail, tile, 0.0)
        real.append(tile)
        low = pltpu.roll(tile_of(count - 1 + k), shift, 1)
        if count + k < total:
            high = pltpu.roll(tile_of(count + k), shift, 1)
            low = jnp.where(lane_of(low.shape) < shift, low, high)
        if k == count - 1:
            low = jnp.where(lane_of(low.shape) < tail, low, 0.0)
        imag.append(low)
    return real, imag


def join_halves(real, imag, half, store):
    count = -(-half // LANES)
    tail = half - (count - 1) * LANES
    total = -(-2 * half // LANES)
    rolled = [pltpu.roll(tile, tail, 1) for tile in imag]
    for k in range(total):
        width = min(LANES, 2 * half - k * LANES)
        if k < count - 1:
            tile = real[k]
        elif k == count - 1:
            tile = jnp.where(lane_of(real[k].shape) < tail, real[k], rolled[0])
        else:
            j = k - count + 1
            tile = rolled[j - 1]
            if j < count:
                tile = jnp.where(lane_of(tile.shape) < tail, tile, rolled[j])
        store(k, width, tile[:, :width])


def select_rows(picker, columns):
    return lax.dot_general(picker, columns, (((1,), (1,)), ((), ())), preferred_element_type=F32)


def gather_kernel(half, keys_hbm, parents_hbm, phase_hbm, leaf_hbm, coarsen_hbm,
                  g1_ref, g2_ref, cc_ref, ss_ref, co_ref, keys_ref, parents_ref, leaf_ref, phase_ref, sems):
    copies = [
        pltpu.make_async_copy(src, dst, sems.at[i])
        for i, (src, dst) in enumerate((
            (keys_hbm, keys_ref), (parents_hbm, parents_ref), (phase_hbm, phase_ref),
            (leaf_hbm, leaf_ref), (coarsen_hbm, co_ref),
        ))
    ]
    for copy in copies:
        copy.start()
    copies[0].wait()
    copies[1].wait()
    parents = parents_ref.shape[1]
    parent_row = jnp.broadcast_to(parents_ref[...].astype(F32), (parents, parents))
    diagonal = lax.broadcasted_iota(jnp.int32, (parents, parents), 0) == lane_of((parents, parents))
    parent_col = jnp.sum(jnp.where(diagonal, parent_row, 0.0), axis=1, keepdims=True).astype(jnp.int32)
    keys = keys_ref[...]
    picks = [
        jnp.where(keys == parent_col * 8 + code, 1.0, 0.0).astype(BF16) for code in range(8)
    ]
    picker = jnp.concatenate(picks, 0)
    copies[2].wait()
    cosine = jnp.cos(phase_ref[...])
    sine = jnp.sin(phase_ref[...])
    cc_ref[:, :half] = cosine
    cc_ref[:, half:] = cosine
    ss_ref[:, :half] = sine
    ss_ref[:, half:] = -sine
    copies[3].wait()
    total = 2 * half
    for start in range(0, total, 256):
        width = min(256, total - start)
        chosen = select_rows(picker, leaf_ref[start : start + width, :])
        first = second = None
        for code in range(8):
            part = chosen[code * parents : (code + 1) * parents]
            a = part * cc_ref[code : code + 1, start : start + width]
            b = part * ss_ref[code : code + 1, start : start + width]
            first = a if first is None else first + a
            second = b if second is None else second + b
        g1_ref[:, start : start + width] = first
        g2_ref[:, start : start + width] = second
    copies[4].wait()


def upward_kernel(half, parents_ref, next_ref, cc_ref, ss_ref, in1_ref, in2_ref, co_ref,
                  up_ref, rows_ref, g1_ref, g2_ref, lhs_ref, row_ref):
    parents = parents_ref.shape[1]
    total = 2 * half
    g1_ref[...] = in1_ref[...]
    g2_ref[...] = in2_ref[...]
    last_parent = parents_ref[:, parents - 1 : parents]
    add1 = add2 = None
    codes = lax.broadcasted_iota(jnp.int32, (8, 1), 0)
    for r in range(next_ref.shape[0]):
        digits = next_ref[r : r + 1, total : total + 3].astype(F32).astype(jnp.int32)
        key = digits[:, 0:1] * 65536 + digits[:, 1:2] * 256 + digits[:, 2:3]
        chosen = jnp.where(key == last_parent * 8 + codes, 1.0, 0.0)
        spectrum = next_ref[r : r + 1, :total].astype(F32)
        a = jnp.sum(chosen * cc_ref[...], axis=0, keepdims=True) * spectrum
        b = jnp.sum(chosen * ss_ref[...], axis=0, keepdims=True) * spectrum
        add1 = a if add1 is None else add1 + a
        add2 = b if add2 is None else add2 + b
    g1_ref[parents - 1 : parents, :total] += add1
    g2_ref[parents - 1 : parents, :total] += add2
    real1, imag1 = split_halves(lambda k: g1_ref[:, k * LANES : (k + 1) * LANES], half)
    real2, imag2 = split_halves(lambda k: g2_ref[:, k * LANES : (k + 1) * LANES], half)
    for k in range(len(real1)):
        lhs_ref[:parents, k * LANES : (k + 1) * LANES] = (real1[k] + imag2[k]).astype(BF16)
        lhs_ref[parents:, k * LANES : (k + 1) * LANES] = (imag1[k] + real2[k]).astype(BF16)
    padded = len(real1) * LANES
    real, imag = [], []
    for start in range(0, padded, 256):
        width = min(256, half - start)
        p0 = jnp.dot(lhs_ref[:, :half], co_ref[0, :, start : start + width], preferred_element_type=F32)
        p1 = jnp.dot(lhs_ref[:, :half], co_ref[1, :, start : start + width], preferred_element_type=F32)
        g1_ref[:, start : start + width] = (p0[:parents] - p1[parents:]).astype(BF16).astype(F32)
        g2_ref[:, start : start + width] = (p1[:parents] + p0[parents:]).astype(BF16).astype(F32)
    for k in range(len(real1)):
        tile1 = g1_ref[:, k * LANES : (k + 1) * LANES]
        tile2 = g2_ref[:, k * LANES : (k + 1) * LANES]
        if k == len(real1) - 1:
            inside = lane_of(tile1.shape) < half - k * LANES
            tile1 = jnp.where(inside, tile1, 0.0)
            tile2 = jnp.where(inside, tile2, 0.0)
        real.append(tile1)
        imag.append(tile2)
        for g in range(parents // 8):
            row_ref[pl.ds(g * 128 + k, 8, stride=16), :] = tile1[g * 8 : g * 8 + 8]
            row_ref[pl.ds(g * 128 + 8 + k, 8, stride=16), :] = tile2[g * 8 : g * 8 + 8]

    def store(k, width, tile):
        up_ref[:, k * LANES : k * LANES + width] = tile.astype(BF16)

    join_halves(real, imag, half, store)
    rows_ref[...] = row_ref[...].reshape(parents, 16, LANES).astype(BF16)


VM = pl.BlockSpec(memory_space=pltpu.VMEM)
SM = pl.BlockSpec(memory_space=pltpu.SMEM)
HB = pl.BlockSpec(memory_space=pltpu.HBM)


def params(mib):
    return pltpu.CompilerParams(vmem_limit_bytes=mib << 20)


def cost(flops, nbytes):
    return pl.CostEstimate(flops=flops, bytes_accessed=nbytes, transcendentals=0)


def in_hbm(value):
    return pltpu.with_memory_space_constraint(value, pltpu.HBM)


def head_kernel(half, keys_hbm, leaf_hbm, head_ref, keys_ref, leaf_ref, sems):
    copies = [
        pltpu.make_async_copy(keys_hbm, keys_ref, sems.at[0]),
        pltpu.make_async_copy(leaf_hbm.at[:, 0:LANES], leaf_ref, sems.at[1]),
    ]
    for copy in copies:
        copy.start()
    total = 2 * half
    count = head_ref.shape[0]
    picker = jnp.where(
        lax.broadcasted_iota(jnp.int32, (16, LANES), 0) == lane_of((16, LANES)), 1.0, 0.0
    ).astype(BF16)
    copies[0].wait()
    for r in range(count):
        key = keys_ref[:, r : r + 1]
        for i, places in enumerate((16, 8, 0)):
            digit = lax.shift_right_logical(key, places) & 255
            head_ref[r : r + 1, total + i : total + i + 1] = digit.astype(F32).astype(BF16)
    copies[1].wait()
    head_ref[:, :total] = select_rows(picker, leaf_ref[...])[:count].astype(BF16)


def leaf_head(leaf_columns, keys_row):
    total = leaf_columns.shape[0]
    return pl.pallas_call(
        lambda *refs: head_kernel(total // 2, *refs),
        out_shape=pltpu.VMEM((2, total + 3), BF16),
        in_specs=[HB, HB],
        out_specs=VM,
        scratch_shapes=[
            pltpu.VMEM(keys_row.shape, jnp.int32),
            pltpu.VMEM((total, LANES), BF16),
            pltpu.SemaphoreType.DMA((2,)),
        ],
        compiler_params=params(2),
        name="leaf_head",
    )(in_hbm(keys_row), in_hbm(leaf_columns))


def gather_leaves(leaf_spectra, leaf_keys, parent_keys, child_phase, coarsen):
    half = child_phase.shape[1]
    leaves = leaf_spectra.shape[1]
    parents = parent_keys.shape[1]
    return pl.pallas_call(
        lambda *refs: gather_kernel(half, *refs),
        out_shape=(
            pltpu.VMEM((parents, 2048), F32),
            pltpu.VMEM((parents, 2048), F32),
            pltpu.VMEM((8, 2 * half), F32),
            pltpu.VMEM((8, 2 * half), F32),
            pltpu.VMEM(coarsen.shape, BF16),
        ),
        in_specs=[HB] * 5,
        out_specs=(VM, VM, VM, VM, VM),
        scratch_shapes=[
            pltpu.VMEM(leaf_keys.shape, jnp.int32),
            pltpu.VMEM(parent_keys.shape, jnp.int32),
            pltpu.VMEM((2 * half, leaves), BF16),
            pltpu.VMEM((8, half), F32),
            pltpu.SemaphoreType.DMA((5,)),
        ],
        compiler_params=params(12),
        cost_estimate=cost(8 << 28, 6 << 20),
        name="gather_leaves",
    )(*map(in_hbm, (leaf_keys, parent_keys, child_phase, leaf_spectra, coarsen)))


def upward_pass(parent_keys, following, cosines, sines, first, second, coarsen):
    half = coarsen.shape[1]
    parents = parent_keys.shape[1]
    return pl.pallas_call(
        lambda *refs: upward_kernel(half, *refs),
        out_shape=(
            jax.ShapeDtypeStruct((parents, 2 * half), BF16),
            pltpu.VMEM((parents, 16, LANES), BF16),
        ),
        in_specs=[VM] * 7,
        out_specs=(VM, VM),
        scratch_shapes=[
            pltpu.VMEM((parents, 2048), F32),
            pltpu.VMEM((parents, 2048), F32),
            pltpu.VMEM((2 * parents, 1024), BF16),
            pltpu.VMEM((parents * 16, LANES), F32),
        ],
        compiler_params=params(12),
        cost_estimate=cost(8 << 28, 6 << 20),
        name="upward_pass",
    )(parent_keys, following, cosines, sines, first, second, coarsen)


def coefficient_kernel(half, transfer_ref, after_ref, coef_ref, wide_ref):
    def lay_out(start, count):
        wide_ref[:count, : 2 * half] = transfer_ref[pl.ds(start, count), :].astype(F32)
        real, imag = split_halves(lambda k: wide_ref[:count, k * LANES : (k + 1) * LANES], half)
        for k in range(len(real)):
            for g in range(0, count, 8):
                size = min(8, count - g)
                coef_ref[pl.ds((start + g) * 16 + k, size, stride=16), :] = real[k][g : g + size]
                coef_ref[pl.ds((start + g) * 16 + 8 + k, size, stride=16), :] = imag[k][g : g + size]

    kinds = transfer_ref.shape[0]
    whole = kinds // 16

    def lay_out_step(i, _):
        lay_out(pl.multiple_of(i * 16, 16), 16)
        return 0

    lax.fori_loop(0, whole, lay_out_step, 0)
    if kinds % 16:
        lay_out(whole * 16, kinds % 16)


def coefficient_rows(transfer, after):
    kinds, width = transfer.shape
    return pl.pallas_call(
        lambda *refs: coefficient_kernel(width // 2, *refs),
        out_shape=pltpu.VMEM((kinds * 16, LANES), F32),
        in_specs=[VM, pl.BlockSpec(memory_space=pl.ANY)],
        out_specs=VM,
        scratch_shapes=[pltpu.VMEM((16, 2048), F32)],
        compiler_params=params(8),
        cost_estimate=cost(8 << 28, 6 << 20),
        name="coefficient_rows",
    )(transfer, after)


def table_kernel(*refs):
    block_refs, table_ref = refs[:HELD], refs[HELD]
    rows = block_refs[0].shape[0]
    odd = lax.rem(lax.axis_index("oct"), 2)
    for w in range(HELD):
        slot = w if w % 2 else w + 2 * odd * (1 - w)
        start = slot * (rows * 16)

        def widen(i, _, w=w, start=start):
            base = pl.multiple_of(start + i * 16, 16)
            table_ref[pl.ds(base, 16), :] = block_refs[w][i].astype(F32)
            return 0

        lax.fori_loop(0, rows, widen, 0, unroll=8)
    table_ref[HELD * rows * 16 : HELD * rows * 16 + 16, :] = jnp.zeros((16, LANES), F32)


def interact_kernel(first, groups, made, index_hbm, steps_hbm, *refs):
    count = 2 * UNROLL
    sems, live_ref, slot_refs = refs[-1], refs[-2], refs[-2 - count : -2]
    refs = refs[: -2 - count]
    per_target = ROW // UNROLL
    size = index_hbm.shape[0] // count
    live_copy = pltpu.make_async_copy(steps_hbm, live_ref, sems.at[len(groups), 0])
    live_copy.start()
    copies = []
    start = 0
    for g, targets in enumerate(groups):
        held, moved = start * per_target, targets * per_target
        copies.append([
            pltpu.make_async_copy(
                index_hbm.at[pl.ds(u * size + first * per_target + held, moved)],
                slot_refs[u].at[pl.ds(held, moved)],
                sems.at[g, u],
            )
            for u in range(count)
        ])
        for copy in copies[-1]:
            copy.start()
        start += targets
    if made:
        coef_ref, table_ref, out_ref = refs
    else:
        coef_ref, out_ref, table_ref = refs[HELD:]
        table_kernel(*refs[:HELD], table_ref)
    live_copy.wait()

    def one_target(j, _):
        base = j * per_target

        def some(at, chunks, sums):
            sums = list(sums)
            for c in range(chunks):
                for u in range(UNROLL):
                    s = pl.multiple_of(slot_refs[u][at + c], 16)
                    t = pl.multiple_of(slot_refs[UNROLL + u][at + c], 16)
                    sr = table_ref[pl.ds(s, 8), :]
                    si = table_ref[pl.ds(s + 8, 8), :]
                    cr = coef_ref[pl.ds(t, 8), :]
                    ci = coef_ref[pl.ds(t + 8, 8), :]
                    p = 2 * (u % 2)
                    sums[p] = sums[p] + (cr * sr - ci * si)
                    sums[p + 1] = sums[p + 1] + (cr * si + ci * sr)
            return tuple(sums)

        chunks = live_ref[first + j]
        pairs = lax.shift_right_logical(chunks, 1)
        sums = (jnp.zeros((8, LANES), F32),) * 4
        sums = lax.fori_loop(0, pairs, lambda i, c: some(base + 2 * i, 2, c), sums)
        sums = lax.fori_loop(0, chunks & 1, lambda i, c: some(base + 2 * pairs, 1, c), sums)
        out_ref[j, 0:8, :] = (sums[0] + sums[2]).astype(out_ref.dtype)
        out_ref[j, 8:16, :] = (sums[1] + sums[3]).astype(out_ref.dtype)
        return 0

    start = 0
    for g, targets in enumerate(groups):
        for copy in copies[g]:
            copy.wait()
        lax.fori_loop(start, start + targets, one_target, 0)
        start += targets


def interact(sources, index, steps, coefs, first, groups, dtype):
    made = not isinstance(sources, list)
    targets = sum(groups)
    out = pltpu.VMEM((targets, 16, LANES), dtype)
    operands = [coefs, sources] if made else [*sources, coefs]
    if not made:
        out = (out, pltpu.VMEM((HELD * sources[0].shape[0] * 16 + 16, LANES), F32))
    return pl.pallas_call(
        lambda *refs: interact_kernel(first, groups, made, *refs),
        out_shape=out,
        in_specs=[pl.BlockSpec(memory_space=pl.ANY)] * 2 + [VM] * len(operands),
        out_specs=VM if made else (VM, VM),
        scratch_shapes=[pltpu.SMEM((targets * (ROW // UNROLL),), jnp.int32)] * (2 * UNROLL)
        + [pltpu.SMEM(steps.shape, jnp.int32), pltpu.SemaphoreType.DMA((len(groups) + 1, 2 * UNROLL))],
        compiler_params=params(12),
        cost_estimate=cost(8 << 30, 6 << 20),
    )(index, steps, *operands)


def finish_kernel(half, near_ref, *refs):
    far_refs, out_ref, sum_ref = refs[:-2], refs[-2], refs[-1]
    targets = out_ref.shape[0]
    start = 0
    for far_ref in far_refs:
        count = far_ref.shape[0]
        sum_ref[start * 16 : (start + count) * 16, :] = (
            near_ref[start : start + count] + far_ref[...].astype(F32)
        ).reshape(count * 16, LANES)
        start += count
    count = -(-half // LANES)
    real, imag = [], []
    for k in range(count):
        real.append(jnp.concatenate([sum_ref[pl.ds(g * 128 + k, 8, stride=16), :] for g in range(targets // 8)], 0))
        imag.append(jnp.concatenate([sum_ref[pl.ds(g * 128 + 8 + k, 8, stride=16), :] for g in range(targets // 8)], 0))

    def store(k, width, tile):
        out_ref[:, k * LANES : k * LANES + width] = tile.astype(BF16)

    join_halves(real, imag, half, store)


def finish(near, fars, half):
    targets = near.shape[0]
    return pl.pallas_call(
        lambda *refs: finish_kernel(half, *refs),
        out_shape=jax.ShapeDtypeStruct((targets, 2 * half), BF16),
        in_specs=[VM] * (1 + len(fars)),
        out_specs=VM,
        scratch_shapes=[pltpu.VMEM((targets * 16, LANES), F32)],
        compiler_params=params(4),
        name="finish",
    )(near, *fars)


def shifted(value, distance):
    count = lax.axis_size("oct")
    return lax.ppermute(value, "oct", [(i, (i + distance) % count) for i in range(count)])


def shards(leaf_spectra, leaf_keys, parent_keys, child_phase, coarsen, transfer, vlist_src, vlist_type):
    count = lax.axis_size("oct")
    half = child_phase.shape[1]
    parents = parent_keys.shape[0]
    keys_row = leaf_keys.reshape(1, -1)
    parents_row = parent_keys.reshape(1, -1)
    leaf_columns = leaf_spectra.T
    head = leaf_head(leaf_columns, keys_row)
    following = lax.ppermute(head, "oct", [(i, i - 1) for i in range(1, count)])
    first, second, cosines, sines, coarsen = gather_leaves(leaf_columns, keys_row, parents_row, child_phase, coarsen)
    upward, rows = upward_pass(parents_row, following, cosines, sines, first, second, coarsen)

    behind2 = shifted(rows, 2)
    crossed = lax.ppermute(rows, "oct", [(i, (i + 1 + 2 * (i % 2)) % count) for i in range(count)])
    swapped = lax.ppermute(behind2, "oct", [(i, i ^ 1) for i in range(count)])
    blocks = [crossed, behind2, swapped, rows]

    packed = jnp.where(vlist_src < 0, DEAD, vlist_src * 512 + vlist_type)
    theirs = shifted(packed, -HELD)
    mine = jnp.where(vlist_src < 0, DEAD, (511 - vlist_src) * 512 + vlist_type)
    ordered = jnp.sort(jnp.concatenate([theirs, mine], 0), axis=1)
    ordered = jnp.pad(ordered, ((0, 0), (0, ROW - ordered.shape[1])), constant_values=DEAD)
    held = HELD * parents
    valid = ordered < held * 512
    steps = (jnp.sum(jnp.where(valid, 1, 0), axis=1).astype(jnp.int32) + (UNROLL - 1)) // UNROLL
    place = ordered >> 9
    is_mine = lax.broadcasted_iota(jnp.int32, place.shape, 0) >= parents
    place = jnp.where(is_mine, held - 1 - place, place)
    place = jnp.where(valid, place, held) * 16
    kind = jnp.where(valid, ordered & 511, 0) * 16

    def columns(table):
        return table.reshape(parents, ROW // UNROLL, UNROLL).transpose(2, 0, 1).reshape(-1)

    far_index = jnp.concatenate([columns(place[:parents]), columns(kind[:parents])])
    near_index = jnp.concatenate([columns(place[parents:]), columns(kind[parents:])])
    coefs = coefficient_rows(transfer, far_index)
    far_steps, near_steps = steps[:parents], steps[parents:]
    cut = parents // 2
    far1, table = interact(blocks, far_index, far_steps, coefs, 0, (8, cut - 8), BF16)
    arrived1 = shifted(far1, HELD)
    far2 = interact(table, far_index, far_steps, coefs, cut, (8, parents - cut - 8), BF16)
    arrived2 = shifted(far2, HELD)
    near = interact(table, near_index, near_steps, coefs, 0, (8, 24, parents - 32), F32)
    local_field = finish(near, [arrived1, arrived2], half)
    return upward, local_field


def solution(mesh):
    return jax.shard_map(
        shards,
        mesh=mesh,
        in_specs=(P("oct", None), P("oct"), P("oct"), P(), P(), P(), P("oct", None), P("oct", None)),
        out_specs=(P("oct", None), P("oct", None)),
        check_vma=False,
    )
```

profile of v0, /device:TPU:1, one launch (start us, length us, event | category | flops | bytes accessed | tf_op | source)
XLA Modules:
  0.0 68.1 jit_solution(8022235601899541285)
XLA Ops:
  0.6 1.4 %leaf_head.1 = bf16[2,2019]{1,0:T(2,128)(2,1)S(1)} custom-call(s32[1,256]{1,0:T(1,128)} %bitcast.23, bf16[2016,256]{1,0:T(8,128)(2,1)} %bitcast.17), custom_call_target="tpu_custom_call" | custom-call | tf_op jit(solution)/shard_map/leaf_head/pallas_call | solution.py:206
  2.0 5.1 %collective-permute-start = (bf16[2,2019]{1,0:T(2,128)(2,1)S(1)}, bf16[2,2019]{1,0:T(2,128)(2,1)S(1)}, u32[]{:S(2)}, u32[]{:S(2)}) collective-permute-start(bf16[2,2019]{1,0:T(2,128)(2,1)S(1)} %leaf_head.1), channel_id=1, source_target_pairs={{1,0},{2,1},{3,2},{4,3},{5,4},{6,5},{7,6},{8,7},{9,8},{10,9},{11,1... | collective-permute-start | bytes 24236 | tf_op jit(solution)/shard_map/ppermute | solution.py:457
  7.1 0.9 %add_select_fusion.1 = (s32[64,189]{1,0:T(8,128)S(1)}, s32[64,189]{1,0:T(8,128)S(1)}) fusion(s32[64,189]{1,0:T(8,128)} %param.15, s32[64,189]{1,0:T(8,128)} %param.14), kind=kLoop, calls=%fused_computation.9 | loop fusion | flops 96768 | bytes 193536 | tf_op jit(solution)/shard_map/jit(_where)/select_n | solution.py:466
  8.0 9.0 %collective-permute-start.1 = (s32[64,189]{1,0:T(8,128)S(1)}, s32[64,189]{1,0:T(8,128)S(1)}, u32[]{:S(2)}, u32[]{:S(2)}) collective-permute-start(s32[64,189]{1,0:T(8,128)S(1)} %get-tuple-element.32), channel_id=1, source_target_pairs={{0,252},{1,253},{2,254},{3,255},{4,0},{5,1},{6,2},{7,3},{8,4},{9,5... | collective-permute-start | bytes 145160 | tf_op jit(solution)/shard_map/ppermute | solution.py:446
  17.0 0.0 copy-start.1
  17.0 2.6 %gather_leaves.1 = (f32[64,2048]{1,0:T(8,128)S(1)}, f32[64,2048]{1,0:T(8,128)S(1)}, f32[8,2016]{1,0:T(8,128)S(1)}, f32[8,2016]{1,0:T(8,128)S(1)}, bf16[2,1008,1008]{2,1,0:T(8,128)(2,1)S(1)}) custom-call(s32[1,256]{1,0:T(1,128)} %bitcast.24, s32[1,64]{1,0:T(1,128)} %bitcast.15, f32[8,1008]{1,0:T(8,128)} %refs_2_.1, bf16[2016,256]{1,0:T(8,128)(2,1)} %bitcast.18, ...), custom_call_target="tpu_custom_call" | custom-call | flops 2147483648 | bytes 6291456 | tf_op jit(solution)/shard_map/gather_leaves/pallas_call | solution.py:225
  19.7 0.0 collective-permute-done.refs_1_
  19.7 0.0 copy-done.1
  19.7 2.0 %upward_pass.1 = (bf16[64,2016]{1,0:T(8,128)(2,1)}, bf16[64,16,128]{2,1,0:T(8,128)(2,1)S(1)}) custom-call(s32[1,64]{1,0:T(1,128)S(1)} %bitcast.16, bf16[2,2019]{1,0:T(2,128)(2,1)S(1)} %collective-permute-done.refs_1_, f32[8,2016]{1,0:T(8,128)S(1)} %get-tuple-element.13.refs_2_, f32[8,2016]{1,0:T(8,128)S(1)} %get-tuple-element.14.refs_3_, ...), custom_call_target="tpu_custom_call" | custom-call | flops 2147483648 | bytes 6291456 | tf_op jit(solution)/shard_map/upward_pass/pallas_call | solution.py:252
  21.6 0.0 collective-permute-start.2
  21.7 0.7 %collective-permute-start.3 = (bf16[64,16,128]{2,1,0:T(8,128)(2,1)S(1)}, bf16[64,16,128]{2,1,0:T(8,128)(2,1)S(1)}, u32[]{:S(2)}, u32[]{:S(2)}) collective-permute-start(bf16[64,16,128]{2,1,0:T(8,128)(2,1)S(1)} %get-tuple-element.20.refs_5_), channel_id=1, source_target_pairs={{0,2},{1,3},{2,4},{3,5},{4,6},{5,7},{6,8},{7,9},{8,10},{9,11},{10,... | collective-permute-start | bytes 786440 | tf_op jit(solution)/shard_map/ppermute | solution.py:446
  22.4 0.0 collective-permute-done.1
  22.4 0.1 copy.22
  22.5 3.3 %sort.15 = (s32[128,189]{0,1:T(8,128)S(1)}, s32[128,189]{0,1:T(8,128)}) sort(s32[128,189]{0,1:T(8,128)S(1)} %copy.22, s32[128,189]{0,1:T(8,128)S(1)} %iota.9.clone), dimensions={1}, to_apply=%region_0.1 | sort | flops 362880 | bytes 387072 | tf_op jit(solution)/shard_map/jit(sort)/sort | solution.py:469
  25.9 0.1 copy.24
  26.0 0.1 select_reduce_fusion
  26.1 0.1 copy.16
  26.2 0.2 copy.17
  26.4 0.0 copy-start
  26.4 0.2 reshape.39
  26.6 0.1 copy.14
  26.7 0.2 copy.15
  27.0 0.2 reshape.37
  27.2 0.1 copy.18
  27.3 0.2 copy.19
  27.5 0.2 reshape.41
  27.7 0.1 copy.20
  27.8 0.2 copy.21
  28.1 0.2 reshape.43
  28.3 13.5 %collective-permute-done.3.refs_3_ = bf16[64,16,128]{2,1,0:T(8,128)(2,1)S(1)} collective-permute-done((bf16[64,16,128]{2,1,0:T(8,128)(2,1)S(1)}, bf16[64,16,128]{2,1,0:T(8,128)(2,1)S(1)}, u32[]{:S(2)}, u32[]{:S(2)}) %collective-permute-start.3) | collective-permute-done | bytes 262176 | tf_op jit(solution)/shard_map/ppermute | solution.py:446
  41.8 0.0 collective-permute-start.4
  41.8 0.0 copy-done
  41.8 2.2 %coefficient_rows.1.refs_6_.refs_2_ = f32[5056,128]{1,0:T(8,128)S(1)} custom-call(bf16[316,2016]{1,0:T(8,128)(2,1)S(1)} %copy-done, s32[32768]{0:T(1024)S(1)} %constant_dynamic-update-slice_fusion.refs_1_.refs_0_), custom_call_target="tpu_custom_call" | custom-call | flops 2147483648 | bytes 6291456 | tf_op jit(solution)/shard_map/coefficient_rows/pallas_call | solution.py:296
  44.0 0.1 fusion.4
  44.1 0.0 collective-permute-done.2.refs_2_
  44.1 0.0 collective-permute-done.4.refs_4_
  44.1 5.9 %shard_map.95 = (bf16[32,16,128]{2,1,0:T(8,128)(2,1)S(1)}, f32[4112,128]{1,0:T(8,128)S(1)}) custom-call(s32[32768]{0:T(1024)S(1)} %constant_dynamic-update-slice_fusion.refs_1_.refs_0_, s32[64]{0:T(128)S(1)} %get-tuple-element.34.refs_1_, bf16[64,16,128]{2,1,0:T(8,128)(2,1)S(1)} %collective-permute-done.2.refs_2_, ...), custom_call_target="tpu_custom_call" | custom-call | flops 8589934592 | bytes 6291456 | tf_op jit(solution)/shard_map/pallas_call | solution.py:397
  50.1 0.1 collective-permute-start.5
  50.2 5.9 %shard_map.97 = bf16[32,16,128]{2,1,0:T(8,128)(2,1)S(1)} custom-call(s32[32768]{0:T(1024)S(1)} %constant_dynamic-update-slice_fusion.refs_1_.refs_0_, s32[64]{0:T(128)S(1)} %get-tuple-element.34.refs_1_, f32[5056,128]{1,0:T(8,128)S(1)} %coefficient_rows.1.refs_6_.refs_2_, f32[4112,128]{1,0:T(8,128)S(1)} %get-tuple-element.21.refs_3_), custom_call_target="tpu_custom_call" | custom-call | flops 8589934592 | bytes 6291456 | tf_op jit(solution)/shard_map/pallas_call | solution.py:397
  56.1 0.1 collective-permute-start.6
  56.2 10.9 %shard_map.96.refs_0_ = f32[64,16,128]{2,1,0:T(8,128)S(1)} custom-call(s32[32768]{0:T(1024)S(1)} %pad_add_fusion.1.refs_0_, s32[64]{0:T(128)S(1)} %get-tuple-element.35.refs_1_, f32[5056,128]{1,0:T(8,128)S(1)} %coefficient_rows.1.refs_6_.refs_2_, f32[4112,128]{1,0:T(8,128)S(1)} %get-tuple-element.21.refs_3_), custom_call_target="tpu_custom_call" | custom-call | flops 8589934592 | bytes 6291456 | tf_op jit(solution)/shard_map/pallas_call | solution.py:397
  67.1 0.0 collective-permute-done.5.refs_1_
  67.1 0.0 collective-permute-done.6.refs_2_
  67.1 0.9 %finish.1 = bf16[64,2016]{1,0:T(8,128)(2,1)} custom-call(f32[64,16,128]{2,1,0:T(8,128)S(1)} %shard_map.96.refs_0_, bf16[32,16,128]{2,1,0:T(8,128)(2,1)S(1)} %collective-permute-done.5.refs_1_, bf16[32,16,128]{2,1,0:T(8,128)(2,1)S(1)} %collective-permute-done.6.refs_2_), custom_call_target="tpu_custom_call" | custom-call | tf_op jit(solution)/shard_map/finish/pallas_call | solution.py:433
  (8 shorter events, 0.1 us)
Async XLA Ops:
  2.0 17.7 %collective-permute-start = (bf16[2,2019]{1,0:T(2,128)(2,1)S(1)}, bf16[2,2019]{1,0:T(2,128)(2,1)S(1)}, u32[]{:S(2)}, u32[]{:S(2)}) collective-permute-start(bf16[2,2019]{1,0:T(2,128)(2,1)S(1)} %leaf_head.1), channel_id=1, source_target_pairs={{1,0},{2,1},{3,2},{4,3},{5,4},{6,5},{7,6},{8,7},{9,8},{10,9},{11,1... | collective-permute-start | bytes 24236 | tf_op jit(solution)/shard_map/ppermute | solution.py:457
  8.0 14.4 %collective-permute-start.1 = (s32[64,189]{1,0:T(8,128)S(1)}, s32[64,189]{1,0:T(8,128)S(1)}, u32[]{:S(2)}, u32[]{:S(2)}) collective-permute-start(s32[64,189]{1,0:T(8,128)S(1)} %get-tuple-element.32), channel_id=1, source_target_pairs={{0,252},{1,253},{2,254},{3,255},{4,0},{5,1},{6,2},{7,3},{8,4},{9,5... | collective-permute-start | bytes 145160 | tf_op jit(solution)/shard_map/ppermute | solution.py:446
  17.0 2.6 %copy-start.1 = (s32[64]{0:T(128)S(1)}, s32[64]{0:T(128)}, u32[]{:S(2)}) copy-start(s32[64]{0:T(128)} %param.10) | copy-start | bytes 772
  21.6 22.5 %collective-permute-start.2 = (bf16[64,16,128]{2,1,0:T(8,128)(2,1)S(1)}, bf16[64,16,128]{2,1,0:T(8,128)(2,1)S(1)}, u32[]{:S(2)}, u32[]{:S(2)}) collective-permute-start(bf16[64,16,128]{2,1,0:T(8,128)(2,1)S(1)} %get-tuple-element.20.refs_5_), channel_id=1, source_target_pairs={{0,1},{1,4},{2,3},{3,6},{4,5},{5,8},{6,7},{7,10},{8,9},{9,12},{10,... | collective-permute-start | bytes 786440 | tf_op jit(solution)/shard_map/ppermute | solution.py:462
  21.7 20.1 %collective-permute-start.3 = (bf16[64,16,128]{2,1,0:T(8,128)(2,1)S(1)}, bf16[64,16,128]{2,1,0:T(8,128)(2,1)S(1)}, u32[]{:S(2)}, u32[]{:S(2)}) collective-permute-start(bf16[64,16,128]{2,1,0:T(8,128)(2,1)S(1)} %get-tuple-element.20.refs_5_), channel_id=1, source_target_pairs={{0,2},{1,3},{2,4},{3,5},{4,6},{5,7},{6,8},{7,9},{8,10},{9,11},{10,... | collective-permute-start | bytes 786440 | tf_op jit(solution)/shard_map/ppermute | solution.py:446
  26.4 15.4 %copy-start = (bf16[316,2016]{1,0:T(8,128)(2,1)S(1)}, bf16[316,2016]{1,0:T(8,128)(2,1)}, u32[]{:S(2)}) copy-start(bf16[316,2016]{1,0:T(8,128)(2,1)} %refs_0_.1) | copy-start | bytes 3822340
  41.8 2.3 %collective-permute-start.4 = (bf16[64,16,128]{2,1,0:T(8,128)(2,1)S(1)}, bf16[64,16,128]{2,1,0:T(8,128)(2,1)S(1)}, u32[]{:S(2)}, u32[]{:S(2)}) collective-permute-start(bf16[64,16,128]{2,1,0:T(8,128)(2,1)S(1)} %collective-permute-done.3.refs_3_), channel_id=1, source_target_pairs={{0,1},{1,0},{2,3},{3,2},{4,5},{5,4},{6,7},{7,6},{8,9},{9,8},{10,11... | collective-permute-start | bytes 786440 | tf_op jit(solution)/shard_map/ppermute | solution.py:463
  50.1 17.0 %collective-permute-start.5 = (bf16[32,16,128]{2,1,0:T(8,128)(2,1)S(1)}, bf16[32,16,128]{2,1,0:T(8,128)(2,1)S(1)}, u32[]{:S(2)}, u32[]{:S(2)}) collective-permute-start(bf16[32,16,128]{2,1,0:T(8,128)(2,1)S(1)} %get-tuple-element.22), channel_id=1, source_target_pairs={{0,4},{1,5},{2,6},{3,7},{4,8},{5,9},{6,10},{7,11},{8,12},{9,13},{1... | collective-permute-start | bytes 393224 | tf_op jit(solution)/shard_map/ppermute | solution.py:446
  56.1 11.0 %collective-permute-start.6 = (bf16[32,16,128]{2,1,0:T(8,128)(2,1)S(1)}, bf16[32,16,128]{2,1,0:T(8,128)(2,1)S(1)}, u32[]{:S(2)}, u32[]{:S(2)}) collective-permute-start(bf16[32,16,128]{2,1,0:T(8,128)(2,1)S(1)} %shard_map.97), channel_id=1, source_target_pairs={{0,4},{1,5},{2,6},{3,7},{4,8},{5,9},{6,10},{7,11},{8,12},{9,13},{1... | collective-permute-start | bytes 393224 | tf_op jit(solution)/shard_map/ppermute | solution.py:446
where the time goes:
time: 68.2 us; the launch traced here: 68.1 us
  Pallas kernels  31.9 us (47%)
  starting transfers between devices  15.1 us (22%)
  waiting for transfers between devices  13.5 us (20%)
  other arithmetic  4.39 us (6%)
  local copies, waits for them, and re-layouts  2.32 us (3%)
  between operations  0.9 us (1%)
    pallas_call x3, Pallas kernels, interact(): pl.pallas_call(lambda *refs: interact_kernel(first, groups, made, *refs),...  22.8 us
    ppermute x4, waiting for transfers between devices, shifted(): lax.ppermute(value, 'oct', [(i, (i + distance) % count) for i in range(co...  13.5 us
    ppermute x4, starting transfers between devices, shifted(): lax.ppermute(value, 'oct', [(i, (i + distance) % count) for i in range(co...  9.94 us
    ppermute x1, starting transfers between devices, shards(): following = lax.ppermute(head, 'oct', [(i, i - 1) for i in range(1, count)])  5.11 us
    sort x1, other arithmetic, shards(): ordered = jnp.sort(jnp.concatenate([theirs, mine], 0), axis=1)  3.34 us
    pallas_call x1, Pallas kernels, gather_leaves(): pl.pallas_call(lambda *refs: gather_kernel(half, *refs), out_shape=(pltpu...  2.59 us
    pallas_call x1, Pallas kernels, coefficient_rows(): pl.pallas_call(lambda *refs: coefficient_kernel(width // 2, *refs), out_s...  2.24 us
    pallas_call x1, Pallas kernels, upward_pass(): pl.pallas_call(lambda *refs: upward_kernel(half, *refs), out_shape=(jax.S...  1.98 us
  transfers between devices with their start and end apart: 7, of which 1 were waited for; matrix products, arithmetic and copies ran while one was open for 10% of the time, Pallas kernels for 35%

commit v1 on v0

--- a/solution.py
+++ b/solution.py
@@ -10,7 +10,8 @@
 BF16 = jnp.bfloat16
 LANES = 128
 HELD = 4
-UNROLL = 16
+SPLIT = 4
+CHUNK = 16
 ROW = 256
 DEAD = 1 << 20
 
@@ -63,13 +64,13 @@
     return lax.dot_general(picker, columns, (((1,), (1,)), ((), ())), preferred_element_type=F32)
 
 
-def gather_kernel(half, keys_hbm, parents_hbm, phase_hbm, leaf_hbm, coarsen_hbm,
-                  g1_ref, g2_ref, cc_ref, ss_ref, co_ref, keys_ref, parents_ref, leaf_ref, phase_ref, sems):
+def gather_kernel(half, keys_hbm, parents_hbm, phase_hbm, leaf_hbm,
+                  g1_ref, g2_ref, cc_ref, ss_ref, keys_ref, parents_ref, leaf_ref, phase_ref, sems):
     copies = [
         pltpu.make_async_copy(src, dst, sems.at[i])
         for i, (src, dst) in enumerate((
             (keys_hbm, keys_ref), (parents_hbm, parents_ref), (phase_hbm, phase_ref),
-            (leaf_hbm, leaf_ref), (coarsen_hbm, co_ref),
+            (leaf_hbm, leaf_ref),
         ))
     ]
     for copy in copies:
@@ -106,7 +107,6 @@
             second = b if second is None else second + b
         g1_ref[:, start : start + width] = first
         g2_ref[:, start : start + width] = second
-    copies[4].wait()
 
 
 def upward_kernel(half, parents_ref, next_ref, cc_ref, ss_ref, in1_ref, in2_ref, co_ref,
@@ -218,7 +218,7 @@
     )(in_hbm(keys_row), in_hbm(leaf_columns))
 
 
-def gather_leaves(leaf_spectra, leaf_keys, parent_keys, child_phase, coarsen):
+def gather_leaves(leaf_spectra, leaf_keys, parent_keys, child_phase):
     half = child_phase.shape[1]
     leaves = leaf_spectra.shape[1]
     parents = parent_keys.shape[1]
@@ -229,21 +229,20 @@
             pltpu.VMEM((parents, 2048), F32),
             pltpu.VMEM((8, 2 * half), F32),
             pltpu.VMEM((8, 2 * half), F32),
-            pltpu.VMEM(coarsen.shape, BF16),
         ),
-        in_specs=[HB] * 5,
-        out_specs=(VM, VM, VM, VM, VM),
+        in_specs=[HB] * 4,
+        out_specs=(VM, VM, VM, VM),
         scratch_shapes=[
             pltpu.VMEM(leaf_keys.shape, jnp.int32),
             pltpu.VMEM(parent_keys.shape, jnp.int32),
             pltpu.VMEM((2 * half, leaves), BF16),
             pltpu.VMEM((8, half), F32),
-            pltpu.SemaphoreType.DMA((5,)),
+            pltpu.SemaphoreType.DMA((4,)),
         ],
         compiler_params=params(12),
         cost_estimate=cost(8 << 28, 6 << 20),
         name="gather_leaves",
-    )(*map(in_hbm, (leaf_keys, parent_keys, child_phase, leaf_spectra, coarsen)))
+    )(*map(in_hbm, (leaf_keys, parent_keys, child_phase, leaf_spectra)))
 
 
 def upward_pass(parent_keys, following, cosines, sines, first, second, coarsen):
@@ -323,10 +322,10 @@
 
 
 def interact_kernel(first, groups, made, index_hbm, steps_hbm, *refs):
-    count = 2 * UNROLL
+    count = 2 * SPLIT
     sems, live_ref, slot_refs = refs[-1], refs[-2], refs[-2 - count : -2]
     refs = refs[: -2 - count]
-    per_target = ROW // UNROLL
+    per_target = ROW // SPLIT
     size = index_hbm.shape[0] // count
     live_copy = pltpu.make_async_copy(steps_hbm, live_ref, sems.at[len(groups), 0])
     live_copy.start()
@@ -342,9 +341,9 @@
             )
             for u in range(count)
         ])
-        for copy in copies[-1]:
-            copy.start()
         start += targets
+    for copy in copies[0]:
+        copy.start()
     if made:
         coef_ref, table_ref, out_ref = refs
     else:
@@ -355,12 +354,12 @@
     def one_target(j, _):
         base = j * per_target
 
-        def some(at, chunks, sums):
+        def some(at, slots, sums):
             sums = list(sums)
-            for c in range(chunks):
-                for u in range(UNROLL):
+            for c in range(slots // SPLIT):
+                for u in range(SPLIT):
                     s = pl.multiple_of(slot_refs[u][at + c], 16)
-                    t = pl.multiple_of(slot_refs[UNROLL + u][at + c], 16)
+                    t = pl.multiple_of(slot_refs[SPLIT + u][at + c], 16)
                     sr = table_ref[pl.ds(s, 8), :]
                     si = table_ref[pl.ds(s + 8, 8), :]
                     cr = coef_ref[pl.ds(t, 8), :]
@@ -373,8 +372,9 @@
         chunks = live_ref[first + j]
         pairs = lax.shift_right_logical(chunks, 1)
         sums = (jnp.zeros((8, LANES), F32),) * 4
-        sums = lax.fori_loop(0, pairs, lambda i, c: some(base + 2 * i, 2, c), sums)
-        sums = lax.fori_loop(0, chunks & 1, lambda i, c: some(base + 2 * pairs, 1, c), sums)
+        width = 2 * CHUNK // SPLIT
+        sums = lax.fori_loop(0, pairs, lambda i, c: some(base + width * i, 2 * CHUNK, c), sums)
+        sums = lax.fori_loop(0, chunks & 1, lambda i, c: some(base + width * pairs, CHUNK, c), sums)
         out_ref[j, 0:8, :] = (sums[0] + sums[2]).astype(out_ref.dtype)
         out_ref[j, 8:16, :] = (sums[1] + sums[3]).astype(out_ref.dtype)
         return 0
@@ -383,6 +383,9 @@
     for g, targets in enumerate(groups):
         for copy in copies[g]:
             copy.wait()
+        if g + 1 < len(groups):
+            for copy in copies[g + 1]:
+                copy.start()
         lax.fori_loop(start, start + targets, one_target, 0)
         start += targets
 
@@ -399,8 +402,8 @@
         out_shape=out,
         in_specs=[pl.BlockSpec(memory_space=pl.ANY)] * 2 + [VM] * len(operands),
         out_specs=VM if made else (VM, VM),
-        scratch_shapes=[pltpu.SMEM((targets * (ROW // UNROLL),), jnp.int32)] * (2 * UNROLL)
-        + [pltpu.SMEM(steps.shape, jnp.int32), pltpu.SemaphoreType.DMA((len(groups) + 1, 2 * UNROLL))],
+        scratch_shapes=[pltpu.SMEM((targets * (ROW // SPLIT),), jnp.int32)] * (2 * SPLIT)
+        + [pltpu.SMEM(steps.shape, jnp.int32), pltpu.SemaphoreType.DMA((len(groups) + 1, 2 * SPLIT))],
         compiler_params=params(12),
         cost_estimate=cost(8 << 30, 6 << 20),
     )(index, steps, *operands)
@@ -455,7 +458,7 @@
     leaf_columns = leaf_spectra.T
     head = leaf_head(leaf_columns, keys_row)
     following = lax.ppermute(head, "oct", [(i, i - 1) for i in range(1, count)])
-    first, second, cosines, sines, coarsen = gather_leaves(leaf_columns, keys_row, parents_row, child_phase, coarsen)
+    first, second, cosines, sines = gather_leaves(leaf_columns, keys_row, parents_row, child_phase)
     upward, rows = upward_pass(parents_row, following, cosines, sines, first, second, coarsen)
 
     behind2 = shifted(rows, 2)
@@ -463,6 +466,7 @@
     swapped = lax.ppermute(behind2, "oct", [(i, i ^ 1) for i in range(count)])
     blocks = [crossed, behind2, swapped, rows]
 
+    vlist_src, vlist_type, _ = lax.optimization_barrier((vlist_src, vlist_type, upward))
     packed = jnp.where(vlist_src < 0, DEAD, vlist_src * 512 + vlist_type)
     theirs = shifted(packed, -HELD)
     mine = jnp.where(vlist_src < 0, DEAD, (511 - vlist_src) * 512 + vlist_type)
@@ -470,7 +474,7 @@
     ordered = jnp.pad(ordered, ((0, 0), (0, ROW - ordered.shape[1])), constant_values=DEAD)
     held = HELD * parents
     valid = ordered < held * 512
-    steps = (jnp.sum(jnp.where(valid, 1, 0), axis=1).astype(jnp.int32) + (UNROLL - 1)) // UNROLL
+    steps = (jnp.sum(jnp.where(valid, 1, 0), axis=1).astype(jnp.int32) + (CHUNK - 1)) // CHUNK
     place = ordered >> 9
     is_mine = lax.broadcasted_iota(jnp.int32, place.shape, 0) >= parents
     place = jnp.where(is_mine, held - 1 - place, place)
@@ -478,18 +482,18 @@
     kind = jnp.where(valid, ordered & 511, 0) * 16
 
     def columns(table):
-        return table.reshape(parents, ROW // UNROLL, UNROLL).transpose(2, 0, 1).reshape(-1)
+        return table.reshape(parents, ROW // SPLIT, SPLIT).transpose(2, 0, 1).reshape(-1)
 
     far_index = jnp.concatenate([columns(place[:parents]), columns(kind[:parents])])
     near_index = jnp.concatenate([columns(place[parents:]), columns(kind[parents:])])
     coefs = coefficient_rows(transfer, far_index)
     far_steps, near_steps = steps[:parents], steps[parents:]
-    cut = parents // 2
-    far1, table = interact(blocks, far_index, far_steps, coefs, 0, (8, cut - 8), BF16)
+    cut = 5 * parents // 8
+    far1, table = interact(blocks, far_index, far_steps, coefs, 0, (8, 16, cut - 24), BF16)
     arrived1 = shifted(far1, HELD)
     far2 = interact(table, far_index, far_steps, coefs, cut, (8, parents - cut - 8), BF16)
     arrived2 = shifted(far2, HELD)
-    near = interact(table, near_index, near_steps, coefs, 0, (8, 24, parents - 32), F32)
+    near = interact(table, near_index, near_steps, coefs, 0, (8, 16, parents - 24), F32)
     local_field = finish(near, [arrived1, arrived2], half)
     return upward, local_field
 

time: 68.2 us -> 68.6 us (level)
  the two profiles are of different devices: /device:TPU:1 before, /device:TPU:32 now
where the time goes in v1:
time: 68.6 us; the launch traced here: 68.5 us
  Pallas kernels  28.8 us (42%)
  waiting for transfers between devices  21 us (31%)
  starting transfers between devices  12.7 us (19%)
  other arithmetic  3.51 us (5%)
  local copies, waits for them, and re-layouts  1.64 us (2%)
  between operations  0.89 us (1%)
    pallas_call x3, Pallas kernels, interact(): pl.pallas_call(lambda *refs: interact_kernel(first, groups, made, *refs),...  20 us
    ppermute x4, waiting for transfers between devices, shifted(): lax.ppermute(value, 'oct', [(i, (i + distance) % count) for i in range(co...  15.8 us
    ppermute x4, starting transfers between devices, shifted(): lax.ppermute(value, 'oct', [(i, (i + distance) % count) for i in range(co...  10.7 us
    ppermute x1, waiting for transfers between devices, shards(): lax.ppermute(rows, 'oct', [(i, (i + 1 + 2 * (i % 2)) % count) for i in ra...  5.17 us
    sort x1, other arithmetic, shards(): ordered = jnp.sort(jnp.concatenate([theirs, mine], 0), axis=1)  3.34 us
    pallas_call x1, Pallas kernels, gather_leaves(): pl.pallas_call(lambda *refs: gather_kernel(half, *refs), out_shape=(pltpu...  2.28 us
    pallas_call x1, Pallas kernels, coefficient_rows(): pl.pallas_call(lambda *refs: coefficient_kernel(width // 2, *refs), out_s...  2.24 us
    pallas_call x1, Pallas kernels, upward_pass(): pl.pallas_call(lambda *refs: upward_kernel(half, *refs), out_shape=(jax.S...  1.96 us
  transfers between devices with their start and end apart: 7, of which 5 were waited for; matrix products, arithmetic and copies ran while one was open for 7% of the time, Pallas kernels for 20%

profile of v1, /device:TPU:32, one launch (start us, length us, event | category | flops | bytes accessed | tf_op | source)
XLA Modules:
  0.0 68.5 jit_solution(15511398506429702454)
XLA Ops:
  0.6 1.4 %leaf_head.1 = bf16[2,2019]{1,0:T(2,128)(2,1)S(1)} custom-call(s32[1,256]{1,0:T(1,128)} %bitcast.23, bf16[2016,256]{1,0:T(8,128)(2,1)} %bitcast.17), custom_call_target="tpu_custom_call" | custom-call | tf_op jit(solution)/shard_map/leaf_head/pallas_call | solution.py:206
  2.0 1.9 %collective-permute-start = (bf16[2,2019]{1,0:T(2,128)(2,1)S(1)}, bf16[2,2019]{1,0:T(2,128)(2,1)S(1)}, u32[]{:S(2)}, u32[]{:S(2)}) collective-permute-start(bf16[2,2019]{1,0:T(2,128)(2,1)S(1)} %leaf_head.1), channel_id=1, source_target_pairs={{1,0},{2,1},{3,2},{4,3},{5,4},{6,5},{7,6},{8,7},{9,8},{10,9},{11,1... | collective-permute-start | bytes 24236 | tf_op jit(solution)/shard_map/ppermute | solution.py:460
  3.9 0.0 copy-start
  3.9 0.0 copy-start.2
  3.9 2.3 %gather_leaves.1 = (f32[64,2048]{1,0:T(8,128)S(1)}, f32[64,2048]{1,0:T(8,128)S(1)}, f32[8,2016]{1,0:T(8,128)S(1)}, f32[8,2016]{1,0:T(8,128)S(1)}) custom-call(s32[1,256]{1,0:T(1,128)} %bitcast.24, s32[1,64]{1,0:T(1,128)} %bitcast.15, f32[8,1008]{1,0:T(8,128)} %refs_2_.1, bf16[2016,256]{1,0:T(8,128)(2,1)} %bitcast.18), custom_call_target="tpu_custom_call" | custom-call | flops 2147483648 | bytes 6291456 | tf_op jit(solution)/shard_map/gather_leaves/pallas_call | solution.py:225
  6.2 0.0 collective-permute-done.refs_1_
  6.2 0.2 copy-done
  6.5 0.0 copy-done.2
  6.5 0.0 copy-start.4
  6.5 2.0 %upward_pass.1 = (bf16[64,2016]{1,0:T(8,128)(2,1)}, bf16[64,16,128]{2,1,0:T(8,128)(2,1)S(1)}) custom-call(s32[1,64]{1,0:T(1,128)S(1)} %bitcast.16, bf16[2,2019]{1,0:T(2,128)(2,1)S(1)} %collective-permute-done.refs_1_, f32[8,2016]{1,0:T(8,128)S(1)} %get-tuple-element.14.refs_2_, f32[8,2016]{1,0:T(8,128)S(1)} %get-tuple-element.15.refs_3_, ...), custom_call_target="tpu_custom_call" | custom-call | flops 2147483648 | bytes 6291456 | tf_op jit(solution)/shard_map/upward_pass/pallas_call | solution.py:251
  8.4 0.0 copy-done.3
  8.4 0.0 copy-done.4
  8.5 0.0 copy-start.1
  8.5 10.6 %collective-permute-start.1 = (s32[64,189]{1,0:T(8,128)S(1)}, s32[64,189]{1,0:T(8,128)S(1)}, u32[]{:S(2)}, u32[]{:S(2)}) collective-permute-start(s32[64,189]{1,0:T(8,128)S(1)} %get-tuple-element.34), channel_id=1, source_target_pairs={{0,252},{1,253},{2,254},{3,255},{4,0},{5,1},{6,2},{7,3},{8,4},{9,5... | collective-permute-start | bytes 145160 | tf_op jit(solution)/shard_map/ppermute | solution.py:449
  19.0 0.0 collective-permute-start.3
  19.0 0.0 collective-permute-start.2
  19.0 1.9 %collective-permute-done.1 = s32[64,189]{1,0:T(8,128)S(1)} collective-permute-done((s32[64,189]{1,0:T(8,128)S(1)}, s32[64,189]{1,0:T(8,128)S(1)}, u32[]{:S(2)}, u32[]{:S(2)}) %collective-permute-start.1) | collective-permute-done | bytes 48416 | tf_op jit(solution)/shard_map/ppermute | solution.py:449
  20.9 0.1 copy.22
  21.1 3.3 %sort.15 = (s32[128,189]{0,1:T(8,128)S(1)}, s32[128,189]{0,1:T(8,128)}) sort(s32[128,189]{0,1:T(8,128)S(1)} %copy.22, s32[128,189]{0,1:T(8,128)S(1)} %iota.9.clone), dimensions={1}, to_apply=%region_0.1 | sort | flops 362880 | bytes 387072 | tf_op jit(solution)/shard_map/jit(sort)/sort | solution.py:473
  24.4 0.1 copy.24
  24.5 0.1 select_reduce_fusion
  24.6 0.1 copy.16
  24.7 0.1 copy.17
  24.9 0.1 reshape.39
  24.9 0.1 copy.14
  25.0 0.1 copy.15
  25.1 0.1 reshape.37
  25.2 0.1 copy.18
  25.3 0.1 copy.19
  25.4 0.1 reshape.41
  25.6 0.1 copy.20
  25.7 0.1 copy.21
  25.8 0.1 reshape.43
  25.9 5.1 %collective-permute-done.3.refs_3_ = bf16[64,16,128]{2,1,0:T(8,128)(2,1)S(1)} collective-permute-done((bf16[64,16,128]{2,1,0:T(8,128)(2,1)S(1)}, bf16[64,16,128]{2,1,0:T(8,128)(2,1)S(1)}, u32[]{:S(2)}, u32[]{:S(2)}) %collective-permute-start.3) | collective-permute-done | bytes 262176 | tf_op jit(solution)/shard_map/ppermute | solution.py:449
  31.0 0.0 collective-permute-start.4
  31.0 0.0 copy-done.1
  31.0 2.2 %coefficient_rows.1.refs_6_.refs_2_ = f32[5056,128]{1,0:T(8,128)S(1)} custom-call(bf16[316,2016]{1,0:T(8,128)(2,1)S(1)} %copy-done.1, s32[32768]{0:T(1024)S(1)} %constant_dynamic-update-slice_fusion.refs_1_.refs_0_), custom_call_target="tpu_custom_call" | custom-call | flops 2147483648 | bytes 6291456 | tf_op jit(solution)/shard_map/coefficient_rows/pallas_call | solution.py:295
  33.3 0.1 fusion.4
  33.3 5.2 %collective-permute-done.2.refs_2_ = bf16[64,16,128]{2,1,0:T(8,128)(2,1)S(1)} collective-permute-done((bf16[64,16,128]{2,1,0:T(8,128)(2,1)S(1)}, bf16[64,16,128]{2,1,0:T(8,128)(2,1)S(1)}, u32[]{:S(2)}, u32[]{:S(2)}) %collective-permute-start.2) | collective-permute-done | bytes 262176 | tf_op jit(solution)/shard_map/ppermute | solution.py:465
  38.5 0.0 collective-permute-done.4.refs_4_
  38.5 6.5 %shard_map.95 = (bf16[40,16,128]{2,1,0:T(8,128)(2,1)S(1)}, f32[4112,128]{1,0:T(8,128)S(1)}) custom-call(s32[32768]{0:T(1024)S(1)} %constant_dynamic-update-slice_fusion.refs_1_.refs_0_, s32[64]{0:T(128)S(1)} %get-tuple-element.36.refs_1_, bf16[64,16,128]{2,1,0:T(8,128)(2,1)S(1)} %collective-permute-done.2.refs_2_, ...), custom_call_target="tpu_custom_call" | custom-call | flops 8589934592 | bytes 6291456 | tf_op jit(solution)/shard_map/pallas_call | solution.py:400
  45.0 4.1 %shard_map.97 = bf16[24,16,128]{2,1,0:T(8,128)(2,1)S(1)} custom-call(s32[32768]{0:T(1024)S(1)} %constant_dynamic-update-slice_fusion.refs_1_.refs_0_, s32[64]{0:T(128)S(1)} %get-tuple-element.36.refs_1_, f32[5056,128]{1,0:T(8,128)S(1)} %coefficient_rows.1.refs_6_.refs_2_, f32[4112,128]{1,0:T(8,128)S(1)} %get-tuple-element.23.refs_3_), custom_call_target="tpu_custom_call" | custom-call | flops 8589934592 | bytes 6291456 | tf_op jit(solution)/shard_map/pallas_call | solution.py:400
  49.1 0.1 collective-permute-start.6
  49.2 0.1 collective-permute-start.5
  49.3 9.4 %shard_map.96.refs_0_ = f32[64,16,128]{2,1,0:T(8,128)S(1)} custom-call(s32[32768]{0:T(1024)S(1)} %pad_add_fusion.1.refs_0_, s32[64]{0:T(128)S(1)} %get-tuple-element.37.refs_1_, f32[5056,128]{1,0:T(8,128)S(1)} %coefficient_rows.1.refs_6_.refs_2_, f32[4112,128]{1,0:T(8,128)S(1)} %get-tuple-element.23.refs_3_), custom_call_target="tpu_custom_call" | custom-call | flops 8589934592 | bytes 6291456 | tf_op jit(solution)/shard_map/pallas_call | solution.py:400
  58.7 7.0 %collective-permute-done.6.refs_2_ = bf16[24,16,128]{2,1,0:T(8,128)(2,1)S(1)} collective-permute-done((bf16[24,16,128]{2,1,0:T(8,128)(2,1)S(1)}, bf16[24,16,128]{2,1,0:T(8,128)(2,1)S(1)}, u32[]{:S(2)}, u32[]{:S(2)}) %collective-permute-start.6) | collective-permute-done | bytes 98336 | tf_op jit(solution)/shard_map/ppermute | solution.py:449
  65.8 1.8 %collective-permute-done.5.refs_1_ = bf16[40,16,128]{2,1,0:T(8,128)(2,1)S(1)} collective-permute-done((bf16[40,16,128]{2,1,0:T(8,128)(2,1)S(1)}, bf16[40,16,128]{2,1,0:T(8,128)(2,1)S(1)}, u32[]{:S(2)}, u32[]{:S(2)}) %collective-permute-start.5) | collective-permute-done | bytes 163872 | tf_op jit(solution)/shard_map/ppermute | solution.py:449
  67.5 0.9 %finish.1 = bf16[64,2016]{1,0:T(8,128)(2,1)} custom-call(f32[64,16,128]{2,1,0:T(8,128)S(1)} %shard_map.96.refs_0_, bf16[40,16,128]{2,1,0:T(8,128)(2,1)S(1)} %collective-permute-done.5.refs_1_, bf16[24,16,128]{2,1,0:T(8,128)(2,1)S(1)} %collective-permute-done.6.refs_2_), custom_call_target="tpu_custom_call" | custom-call | tf_op jit(solution)/shard_map/finish/pallas_call | solution.py:436
  (10 shorter events, 0.1 us)
Async XLA Ops:
  2.0 4.2 %collective-permute-start = (bf16[2,2019]{1,0:T(2,128)(2,1)S(1)}, bf16[2,2019]{1,0:T(2,128)(2,1)S(1)}, u32[]{:S(2)}, u32[]{:S(2)}) collective-permute-start(bf16[2,2019]{1,0:T(2,128)(2,1)S(1)} %leaf_head.1), channel_id=1, source_target_pairs={{1,0},{2,1},{3,2},{4,3},{5,4},{6,5},{7,6},{8,7},{9,8},{10,9},{11,1... | collective-permute-start | bytes 24236 | tf_op jit(solution)/shard_map/ppermute | solution.py:460
  3.9 2.5 %copy-start = (bf16[2,1008,1008]{2,1,0:T(8,128)(2,1)S(1)}, bf16[2,1008,1008]{2,1,0:T(8,128)(2,1)}, u32[]{:S(2)}) copy-start(bf16[2,1008,1008]{2,1,0:T(8,128)(2,1)} %refs_6_.1) | copy-start | bytes 12192772
  3.9 2.5 %copy-start.2 = (s32[64]{0:T(128)S(1)}, s32[64]{0:T(128)}, u32[]{:S(2)}) copy-start(s32[64]{0:T(128)} %param.10) | copy-start | bytes 772
  6.5 2.0 %copy-start.3 = (s32[64,189]{1,0:T(8,128)S(1)}, s32[64,189]{1,0:T(8,128)}, u32[]{:S(2)}) copy-start(s32[64,189]{1,0:T(8,128)} %param.15) | copy-start | bytes 145156
  6.5 2.0 %copy-start.4 = (s32[64,189]{1,0:T(8,128)S(1)}, s32[64,189]{1,0:T(8,128)}, u32[]{:S(2)}) copy-start(s32[64,189]{1,0:T(8,128)} %param.14) | copy-start | bytes 145156
  8.5 22.6 %copy-start.1 = (bf16[316,2016]{1,0:T(8,128)(2,1)S(1)}, bf16[316,2016]{1,0:T(8,128)(2,1)}, u32[]{:S(2)}) copy-start(bf16[316,2016]{1,0:T(8,128)(2,1)} %refs_0_.1) | copy-start | bytes 3822340
  8.5 12.5 %collective-permute-start.1 = (s32[64,189]{1,0:T(8,128)S(1)}, s32[64,189]{1,0:T(8,128)S(1)}, u32[]{:S(2)}, u32[]{:S(2)}) collective-permute-start(s32[64,189]{1,0:T(8,128)S(1)} %get-tuple-element.34), channel_id=1, source_target_pairs={{0,252},{1,253},{2,254},{3,255},{4,0},{5,1},{6,2},{7,3},{8,4},{9,5... | collective-permute-start | bytes 145160 | tf_op jit(solution)/shard_map/ppermute | solution.py:449
  19.0 12.0 %collective-permute-start.3 = (bf16[64,16,128]{2,1,0:T(8,128)(2,1)S(1)}, bf16[64,16,128]{2,1,0:T(8,128)(2,1)S(1)}, u32[]{:S(2)}, u32[]{:S(2)}) collective-permute-start(bf16[64,16,128]{2,1,0:T(8,128)(2,1)S(1)} %get-tuple-element.22.refs_5_), channel_id=1, source_target_pairs={{0,2},{1,3},{2,4},{3,5},{4,6},{5,7},{6,8},{7,9},{8,10},{9,11},{10,... | collective-permute-start | bytes 786440 | tf_op jit(solution)/shard_map/ppermute | solution.py:449
  19.0 19.5 %collective-permute-start.2 = (bf16[64,16,128]{2,1,0:T(8,128)(2,1)S(1)}, bf16[64,16,128]{2,1,0:T(8,128)(2,1)S(1)}, u32[]{:S(2)}, u32[]{:S(2)}) collective-permute-start(bf16[64,16,128]{2,1,0:T(8,128)(2,1)S(1)} %get-tuple-element.22.refs_5_), channel_id=1, source_target_pairs={{0,1},{1,4},{2,3},{3,6},{4,5},{5,8},{6,7},{7,10},{8,9},{9,12},{10,... | collective-permute-start | bytes 786440 | tf_op jit(solution)/shard_map/ppermute | solution.py:465
  31.0 7.5 %collective-permute-start.4 = (bf16[64,16,128]{2,1,0:T(8,128)(2,1)S(1)}, bf16[64,16,128]{2,1,0:T(8,128)(2,1)S(1)}, u32[]{:S(2)}, u32[]{:S(2)}) collective-permute-start(bf16[64,16,128]{2,1,0:T(8,128)(2,1)S(1)} %collective-permute-done.3.refs_3_), channel_id=1, source_target_pairs={{0,1},{1,0},{2,3},{3,2},{4,5},{5,4},{6,7},{7,6},{8,9},{9,8},{10,11... | collective-permute-start | bytes 786440 | tf_op jit(solution)/shard_map/ppermute | solution.py:466
  49.1 16.6 %collective-permute-start.6 = (bf16[24,16,128]{2,1,0:T(8,128)(2,1)S(1)}, bf16[24,16,128]{2,1,0:T(8,128)(2,1)S(1)}, u32[]{:S(2)}, u32[]{:S(2)}) collective-permute-start(bf16[24,16,128]{2,1,0:T(8,128)(2,1)S(1)} %shard_map.97), channel_id=1, source_target_pairs={{0,4},{1,5},{2,6},{3,7},{4,8},{5,9},{6,10},{7,11},{8,12},{9,13},{1... | collective-permute-start | bytes 294920 | tf_op jit(solution)/shard_map/ppermute | solution.py:449
  49.2 18.3 %collective-permute-start.5 = (bf16[40,16,128]{2,1,0:T(8,128)(2,1)S(1)}, bf16[40,16,128]{2,1,0:T(8,128)(2,1)S(1)}, u32[]{:S(2)}, u32[]{:S(2)}) collective-permute-start(bf16[40,16,128]{2,1,0:T(8,128)(2,1)S(1)} %get-tuple-element.24), channel_id=1, source_target_pairs={{0,4},{1,5},{2,6},{3,7},{4,8},{5,9},{6,10},{7,11},{8,12},{9,13},{1... | collective-permute-start | bytes 491528 | tf_op jit(solution)/shard_map/ppermute | solution.py:449

commit v2 on v1

--- a/solution.py
+++ b/solution.py
@@ -64,19 +64,10 @@
     return lax.dot_general(picker, columns, (((1,), (1,)), ((), ())), preferred_element_type=F32)
 
 
-def gather_kernel(half, keys_hbm, parents_hbm, phase_hbm, leaf_hbm,
-                  g1_ref, g2_ref, cc_ref, ss_ref, keys_ref, parents_ref, leaf_ref, phase_ref, sems):
-    copies = [
-        pltpu.make_async_copy(src, dst, sems.at[i])
-        for i, (src, dst) in enumerate((
-            (keys_hbm, keys_ref), (parents_hbm, parents_ref), (phase_hbm, phase_ref),
-            (leaf_hbm, leaf_ref),
-        ))
-    ]
-    for copy in copies:
-        copy.start()
-    copies[0].wait()
-    copies[1].wait()
+def gather_kernel(half, keys_ref, parents_ref, phase_ref, leaf_ref, coarsen_hbm,
+                  g1_ref, g2_ref, cc_ref, ss_ref, co_ref, sem):
+    copy = pltpu.make_async_copy(coarsen_hbm.at[0], co_ref, sem)
+    copy.start()
     parents = parents_ref.shape[1]
     parent_row = jnp.broadcast_to(parents_ref[...].astype(F32), (parents, parents))
     diagonal = lax.broadcasted_iota(jnp.int32, (parents, parents), 0) == lane_of((parents, parents))
@@ -86,14 +77,12 @@
         jnp.where(keys == parent_col * 8 + code, 1.0, 0.0).astype(BF16) for code in range(8)
     ]
     picker = jnp.concatenate(picks, 0)
-    copies[2].wait()
     cosine = jnp.cos(phase_ref[...])
     sine = jnp.sin(phase_ref[...])
     cc_ref[:, :half] = cosine
     cc_ref[:, half:] = cosine
     ss_ref[:, :half] = sine
     ss_ref[:, half:] = -sine
-    copies[3].wait()
     total = 2 * half
     for start in range(0, total, 256):
         width = min(256, total - start)
@@ -107,10 +96,13 @@
             second = b if second is None else second + b
         g1_ref[:, start : start + width] = first
         g2_ref[:, start : start + width] = second
-
-
-def upward_kernel(half, parents_ref, next_ref, cc_ref, ss_ref, in1_ref, in2_ref, co_ref,
-                  up_ref, rows_ref, g1_ref, g2_ref, lhs_ref, row_ref):
+    copy.wait()
+
+
+def upward_kernel(half, parents_ref, next_ref, cc_ref, ss_ref, in1_ref, in2_ref, co_ref, coarsen_hbm,
+                  up_ref, rows_ref, g1_ref, g2_ref, lhs_ref, row_ref, co_imag_ref, sem):
+    copy = pltpu.make_async_copy(coarsen_hbm.at[1], co_imag_ref, sem)
+    copy.start()
     parents = parents_ref.shape[1]
     total = 2 * half
     g1_ref[...] = in1_ref[...]
@@ -134,12 +126,13 @@
     for k in range(len(real1)):
         lhs_ref[:parents, k * LANES : (k + 1) * LANES] = (real1[k] + imag2[k]).astype(BF16)
         lhs_ref[parents:, k * LANES : (k + 1) * LANES] = (imag1[k] + real2[k]).astype(BF16)
+    copy.wait()
     padded = len(real1) * LANES
     real, imag = [], []
     for start in range(0, padded, 256):
         width = min(256, half - start)
-        p0 = jnp.dot(lhs_ref[:, :half], co_ref[0, :, start : start + width], preferred_element_type=F32)
-        p1 = jnp.dot(lhs_ref[:, :half], co_ref[1, :, start : start + width], preferred_element_type=F32)
+        p0 = jnp.dot(lhs_ref[:, :half], co_ref[:, start : start + width], preferred_element_type=F32)
+        p1 = jnp.dot(lhs_ref[:, :half], co_imag_ref[:, start : start + width], preferred_element_type=F32)
         g1_ref[:, start : start + width] = (p0[:parents] - p1[parents:]).astype(BF16).astype(F32)
         g2_ref[:, start : start + width] = (p1[:parents] + p0[parents:]).astype(BF16).astype(F32)
     for k in range(len(real1)):
@@ -179,10 +172,13 @@
     return pltpu.with_memory_space_constraint(value, pltpu.HBM)
 
 
-def head_kernel(half, keys_hbm, leaf_hbm, head_ref, keys_ref, leaf_ref, sems):
+def head_kernel(half, keys_hbm, parents_hbm, phase_hbm, leaf_hbm,
+                head_ref, keys_ref, parents_ref, phase_ref, leaf_ref, sems):
     copies = [
-        pltpu.make_async_copy(keys_hbm, keys_ref, sems.at[0]),
-        pltpu.make_async_copy(leaf_hbm.at[:, 0:LANES], leaf_ref, sems.at[1]),
+        pltpu.make_async_copy(src, dst, sems.at[i])
+        for i, (src, dst) in enumerate((
+            (leaf_hbm, leaf_ref), (keys_hbm, keys_ref), (parents_hbm, parents_ref), (phase_hbm, phase_ref),
+        ))
     ]
     for copy in copies:
         copy.start()
@@ -191,36 +187,34 @@
     picker = jnp.where(
         lax.broadcasted_iota(jnp.int32, (16, LANES), 0) == lane_of((16, LANES)), 1.0, 0.0
     ).astype(BF16)
-    copies[0].wait()
+    copies[1].wait()
     for r in range(count):
         key = keys_ref[:, r : r + 1]
         for i, places in enumerate((16, 8, 0)):
             digit = lax.shift_right_logical(key, places) & 255
             head_ref[r : r + 1, total + i : total + i + 1] = digit.astype(F32).astype(BF16)
-    copies[1].wait()
-    head_ref[:, :total] = select_rows(picker, leaf_ref[...])[:count].astype(BF16)
-
-
-def leaf_head(leaf_columns, keys_row):
+    copies[2].wait()
+    copies[3].wait()
+    copies[0].wait()
+    head_ref[:, :total] = select_rows(picker, leaf_ref[:, 0:LANES])[:count].astype(BF16)
+
+
+def leaf_head(keys_row, parents_row, child_phase, leaf_columns):
     total = leaf_columns.shape[0]
+    operands = (keys_row, parents_row, child_phase, leaf_columns)
     return pl.pallas_call(
         lambda *refs: head_kernel(total // 2, *refs),
-        out_shape=pltpu.VMEM((2, total + 3), BF16),
-        in_specs=[HB, HB],
-        out_specs=VM,
-        scratch_shapes=[
-            pltpu.VMEM(keys_row.shape, jnp.int32),
-            pltpu.VMEM((total, LANES), BF16),
-            pltpu.SemaphoreType.DMA((2,)),
-        ],
-        compiler_params=params(2),
+        out_shape=(pltpu.VMEM((2, total + 3), BF16), *(pltpu.VMEM(x.shape, x.dtype) for x in operands)),
+        in_specs=[HB] * 4,
+        out_specs=(VM,) * 5,
+        scratch_shapes=[pltpu.SemaphoreType.DMA((4,))],
+        compiler_params=params(4),
         name="leaf_head",
-    )(in_hbm(keys_row), in_hbm(leaf_columns))
-
-
-def gather_leaves(leaf_spectra, leaf_keys, parent_keys, child_phase):
+    )(*map(in_hbm, operands))
+
+
+def gather_leaves(leaf_spectra, leaf_keys, parent_keys, child_phase, coarsen):
     half = child_phase.shape[1]
-    leaves = leaf_spectra.shape[1]
     parents = parent_keys.shape[1]
     return pl.pallas_call(
         lambda *refs: gather_kernel(half, *refs),
@@ -229,23 +223,18 @@
             pltpu.VMEM((parents, 2048), F32),
             pltpu.VMEM((8, 2 * half), F32),
             pltpu.VMEM((8, 2 * half), F32),
+            pltpu.VMEM((half, half), BF16),
         ),
-        in_specs=[HB] * 4,
-        out_specs=(VM, VM, VM, VM),
-        scratch_shapes=[
-            pltpu.VMEM(leaf_keys.shape, jnp.int32),
-            pltpu.VMEM(parent_keys.shape, jnp.int32),
-            pltpu.VMEM((2 * half, leaves), BF16),
-            pltpu.VMEM((8, half), F32),
-            pltpu.SemaphoreType.DMA((4,)),
-        ],
+        in_specs=[VM] * 4 + [HB],
+        out_specs=(VM,) * 5,
+        scratch_shapes=[pltpu.SemaphoreType.DMA],
         compiler_params=params(12),
         cost_estimate=cost(8 << 28, 6 << 20),
         name="gather_leaves",
-    )(*map(in_hbm, (leaf_keys, parent_keys, child_phase, leaf_spectra)))
-
-
-def upward_pass(parent_keys, following, cosines, sines, first, second, coarsen):
+    )(leaf_keys, parent_keys, child_phase, leaf_spectra, in_hbm(coarsen))
+
+
+def upward_pass(parent_keys, following, cosines, sines, first, second, coarsen_real, coarsen):
     half = coarsen.shape[1]
     parents = parent_keys.shape[1]
     return pl.pallas_call(
@@ -254,18 +243,20 @@
             jax.ShapeDtypeStruct((parents, 2 * half), BF16),
             pltpu.VMEM((parents, 16, LANES), BF16),
         ),
-        in_specs=[VM] * 7,
+        in_specs=[VM] * 7 + [HB],
         out_specs=(VM, VM),
         scratch_shapes=[
             pltpu.VMEM((parents, 2048), F32),
             pltpu.VMEM((parents, 2048), F32),
             pltpu.VMEM((2 * parents, 1024), BF16),
             pltpu.VMEM((parents * 16, LANES), F32),
+            pltpu.VMEM((half, half), BF16),
+            pltpu.SemaphoreType.DMA,
         ],
         compiler_params=params(12),
         cost_estimate=cost(8 << 28, 6 << 20),
         name="upward_pass",
-    )(parent_keys, following, cosines, sines, first, second, coarsen)
+    )(parent_keys, following, cosines, sines, first, second, coarsen_real, in_hbm(coarsen))
 
 
 def coefficient_kernel(half, transfer_ref, after_ref, coef_ref, wide_ref):
@@ -456,10 +447,14 @@
     keys_row = leaf_keys.reshape(1, -1)
     parents_row = parent_keys.reshape(1, -1)
     leaf_columns = leaf_spectra.T
-    head = leaf_head(leaf_columns, keys_row)
+    head, keys_row, parents_row, child_phase, leaf_columns = leaf_head(
+        keys_row, parents_row, child_phase, leaf_columns
+    )
     following = lax.ppermute(head, "oct", [(i, i - 1) for i in range(1, count)])
-    first, second, cosines, sines = gather_leaves(leaf_columns, keys_row, parents_row, child_phase)
-    upward, rows = upward_pass(parents_row, following, cosines, sines, first, second, coarsen)
+    first, second, cosines, sines, coarsen_real = gather_leaves(
+        leaf_columns, keys_row, parents_row, child_phase, coarsen
+    )
+    upward, rows = upward_pass(parents_row, following, cosines, sines, first, second, coarsen_real, coarsen)
 
     behind2 = shifted(rows, 2)
     crossed = lax.ppermute(rows, "oct", [(i, (i + 1 + 2 * (i % 2)) % count) for i in range(count)])

time: 68.6 us -> 69.5 us (1.013)
  Pallas kernels: 28.8 us -> 29.6 us
    ppermute x1, waiting for transfers between devices: 5.17 us -> 8.51 us  [shards(): lax.ppermute(rows, 'oct', [(i, (i + 1 + 2 * (i % 2)) % count) for i in ra...]
    ppermute x4, waiting for transfers between devices: 15.8 us -> 12.6 us  [shifted(): lax.ppermute(value, 'oct', [(i, (i + distance) % count) for i in range(co...]
    pallas_call x1, Pallas kernels: 1.96 us -> 3.31 us  [upward_pass(): pl.pallas_call(lambda *refs: upward_kernel(half, *refs), out_shape=(jax.S...]
  transfers between devices with their start and end apart: 7 -> 7, of which waited for: 5 -> 5; matrix products, arithmetic and copies ran while one was open for 7% -> 7% of each run, Pallas kernels for 20% -> 19%
where the time goes in v2:
time: 69.5 us; the launch traced here: 69.3 us
  Pallas kernels  29.6 us (43%)
  waiting for transfers between devices  21.2 us (31%)
  starting transfers between devices  12.7 us (18%)
  other arithmetic  3.52 us (5%)
  local copies, waits for them, and re-layouts  1.43 us (2%)
  between operations  0.91 us (1%)
    pallas_call x3, Pallas kernels, interact(): pl.pallas_call(lambda *refs: interact_kernel(first, groups, made, *refs),...  20 us
    ppermute x4, waiting for transfers between devices, shifted(): lax.ppermute(value, 'oct', [(i, (i + distance) % count) for i in range(co...  12.6 us
    ppermute x4, starting transfers between devices, shifted(): lax.ppermute(value, 'oct', [(i, (i + distance) % count) for i in range(co...  10.7 us
    ppermute x1, waiting for transfers between devices, shards(): lax.ppermute(rows, 'oct', [(i, (i + 1 + 2 * (i % 2)) % count) for i in ra...  8.51 us
    sort x1, other arithmetic, shards(): ordered = jnp.sort(jnp.concatenate([theirs, mine], 0), axis=1)  3.34 us
    pallas_call x1, Pallas kernels, upward_pass(): pl.pallas_call(lambda *refs: upward_kernel(half, *refs), out_shape=(jax.S...  3.31 us
    pallas_call x1, Pallas kernels, coefficient_rows(): pl.pallas_call(lambda *refs: coefficient_kernel(width // 2, *refs), out_s...  2.24 us
    ppermute x1, starting transfers between devices, shards(): following = lax.ppermute(head, 'oct', [(i, i - 1) for i in range(1, count)])  1.92 us
  transfers between devices with their start and end apart: 7, of which 5 were waited for; matrix products, arithmetic and copies ran while one was open for 7% of the time, Pallas kernels for 19%

profile of v2, /device:TPU:32, one launch (start us, length us, event | category | flops | bytes accessed | tf_op | source)
XLA Modules:
  0.0 69.3 jit_solution(1782986749121626056)
XLA Ops:
  0.6 1.5 %leaf_head.1 = (bf16[2,2019]{1,0:T(2,128)(2,1)S(1)}, s32[1,256]{1,0:T(1,128)S(1)}, s32[1,64]{1,0:T(1,128)S(1)}, f32[8,1008]{1,0:T(8,128)S(1)}, bf16[2016,256]{1,0:T(8,128)(2,1)S(1)}) custom-call(s32[1,256]{1,0:T(1,128)} %bitcast.20, s32[1,64]{1,0:T(1,128)} %bitcast.21, f32[8,1008]{1,0:T(8,128)} %refs_2_.1, bf16[2016,256]{1,0:T(8,128)(2,1)} %bitcast.15), custom_call_target="tpu_custom_call" | custom-call | tf_op jit(solution)/shard_map/leaf_head/pallas_call | solution.py:205
  2.2 1.9 %collective-permute-start = (bf16[2,2019]{1,0:T(2,128)(2,1)S(1)}, bf16[2,2019]{1,0:T(2,128)(2,1)S(1)}, u32[]{:S(2)}, u32[]{:S(2)}) collective-permute-start(bf16[2,2019]{1,0:T(2,128)(2,1)S(1)} %get-tuple-element.21), channel_id=1, source_target_pairs={{1,0},{2,1},{3,2},{4,3},{5,4},{6,5},{7,6},{8,7},{9,8},{10,9},{11,1... | collective-permute-start | bytes 24236 | tf_op jit(solution)/shard_map/ppermute | solution.py:453
  4.1 1.6 %gather_leaves.1 = (f32[64,2048]{1,0:T(8,128)S(1)}, f32[64,2048]{1,0:T(8,128)S(1)}, f32[8,2016]{1,0:T(8,128)S(1)}, f32[8,2016]{1,0:T(8,128)S(1)}, bf16[1008,1008]{1,0:T(8,128)(2,1)S(1)}) custom-call(s32[1,256]{1,0:T(1,128)S(1)} %get-tuple-element.22.refs_0_, s32[1,64]{1,0:T(1,128)S(1)} %get-tuple-element.20.refs_1_.refs_0_, ...), custom_call_target="tpu_custom_call" | custom-call | flops 2147483648 | bytes 6291456 | tf_op jit(solution)/shard_map/gather_leaves/pallas_call | solution.py:219
  5.7 0.0 collective-permute-done.refs_1_
  5.7 0.0 copy-start.1
  5.7 0.0 copy-start.2
  5.8 3.3 %upward_pass.1 = (bf16[64,2016]{1,0:T(8,128)(2,1)}, bf16[64,16,128]{2,1,0:T(8,128)(2,1)S(1)}) custom-call(s32[1,64]{1,0:T(1,128)S(1)} %get-tuple-element.20.refs_1_.refs_0_, bf16[2,2019]{1,0:T(2,128)(2,1)S(1)} %collective-permute-done.refs_1_, f32[8,2016]{1,0:T(8,128)S(1)} %get-tuple-element.25.refs_2_, f32[8,2016]{1,0:T(8,128)S(1)} %get-tuple-element.26.refs_3_, ...), custom_call_target="tpu_custom_call" | custom-call | flops 2147483648 | bytes 6291456 | tf_op jit(solution)/shard_map/upward_pass/pallas_call | solution.py:240
  9.1 0.0 copy-done.1
  9.1 0.0 copy-done.2
  9.1 10.6 %collective-permute-start.1 = (s32[64,189]{1,0:T(8,128)S(1)}, s32[64,189]{1,0:T(8,128)S(1)}, u32[]{:S(2)}, u32[]{:S(2)}) collective-permute-start(s32[64,189]{1,0:T(8,128)S(1)} %get-tuple-element.46), channel_id=1, source_target_pairs={{0,252},{1,253},{2,254},{3,255},{4,0},{5,1},{6,2},{7,3},{8,4},{9,5... | collective-permute-start | bytes 145160 | tf_op jit(solution)/shard_map/ppermute | solution.py:440
  19.7 0.0 collective-permute-start.3
  19.7 0.0 collective-permute-start.2
  19.7 1.9 %collective-permute-done.1 = s32[64,189]{1,0:T(8,128)S(1)} collective-permute-done((s32[64,189]{1,0:T(8,128)S(1)}, s32[64,189]{1,0:T(8,128)S(1)}, u32[]{:S(2)}, u32[]{:S(2)}) %collective-permute-start.1) | collective-permute-done | bytes 48416 | tf_op jit(solution)/shard_map/ppermute | solution.py:440
  21.6 0.1 copy.22
  21.7 3.3 %sort.15 = (s32[128,189]{0,1:T(8,128)S(1)}, s32[128,189]{0,1:T(8,128)}) sort(s32[128,189]{0,1:T(8,128)S(1)} %copy.22, s32[128,189]{0,1:T(8,128)S(1)} %iota.9.clone), dimensions={1}, to_apply=%region_0.1 | sort | flops 362880 | bytes 387072 | tf_op jit(solution)/shard_map/jit(sort)/sort | solution.py:468
  25.1 0.0 copy-start
  25.1 0.1 copy.24
  25.2 0.1 select_reduce_fusion
  25.3 0.1 copy.16
  25.4 0.1 copy.17
  25.5 0.1 reshape.39
  25.6 0.1 copy.14
  25.7 0.1 copy.15
  25.8 0.1 reshape.37
  25.9 0.1 copy.18
  26.0 0.1 copy.19
  26.1 0.1 reshape.41
  26.3 0.1 copy.20
  26.4 0.1 copy.21
  26.5 0.1 reshape.43
  26.6 2.5 %collective-permute-done.3.refs_3_ = bf16[64,16,128]{2,1,0:T(8,128)(2,1)S(1)} collective-permute-done((bf16[64,16,128]{2,1,0:T(8,128)(2,1)S(1)}, bf16[64,16,128]{2,1,0:T(8,128)(2,1)S(1)}, u32[]{:S(2)}, u32[]{:S(2)}) %collective-permute-start.3) | collective-permute-done | bytes 262176 | tf_op jit(solution)/shard_map/ppermute | solution.py:440
  29.1 0.0 collective-permute-start.4
  29.1 0.0 copy-done
  29.1 2.2 %coefficient_rows.1.refs_6_.refs_2_ = f32[5056,128]{1,0:T(8,128)S(1)} custom-call(bf16[316,2016]{1,0:T(8,128)(2,1)S(1)} %copy-done, s32[32768]{0:T(1024)S(1)} %constant_dynamic-update-slice_fusion.refs_1_.refs_0_), custom_call_target="tpu_custom_call" | custom-call | flops 2147483648 | bytes 6291456 | tf_op jit(solution)/shard_map/coefficient_rows/pallas_call | solution.py:286
  31.3 0.1 fusion.4
  31.4 8.5 %collective-permute-done.2.refs_2_ = bf16[64,16,128]{2,1,0:T(8,128)(2,1)S(1)} collective-permute-done((bf16[64,16,128]{2,1,0:T(8,128)(2,1)S(1)}, bf16[64,16,128]{2,1,0:T(8,128)(2,1)S(1)}, u32[]{:S(2)}, u32[]{:S(2)}) %collective-permute-start.2) | collective-permute-done | bytes 262176 | tf_op jit(solution)/shard_map/ppermute | solution.py:460
  39.9 0.0 collective-permute-done.4.refs_4_
  39.9 6.5 %shard_map.95 = (bf16[40,16,128]{2,1,0:T(8,128)(2,1)S(1)}, f32[4112,128]{1,0:T(8,128)S(1)}) custom-call(s32[32768]{0:T(1024)S(1)} %constant_dynamic-update-slice_fusion.refs_1_.refs_0_, s32[64]{0:T(128)S(1)} %get-tuple-element.48.refs_1_, bf16[64,16,128]{2,1,0:T(8,128)(2,1)S(1)} %collective-permute-done.2.refs_2_, ...), custom_call_target="tpu_custom_call" | custom-call | flops 8589934592 | bytes 6291456 | tf_op jit(solution)/shard_map/pallas_call | solution.py:391
  46.4 4.1 %shard_map.97 = bf16[24,16,128]{2,1,0:T(8,128)(2,1)S(1)} custom-call(s32[32768]{0:T(1024)S(1)} %constant_dynamic-update-slice_fusion.refs_1_.refs_0_, s32[64]{0:T(128)S(1)} %get-tuple-element.48.refs_1_, f32[5056,128]{1,0:T(8,128)S(1)} %coefficient_rows.1.refs_6_.refs_2_, f32[4112,128]{1,0:T(8,128)S(1)} %get-tuple-element.35.refs_3_), custom_call_target="tpu_custom_call" | custom-call | flops 8589934592 | bytes 6291456 | tf_op jit(solution)/shard_map/pallas_call | solution.py:391
  50.5 0.1 collective-permute-start.6
  50.6 0.1 collective-permute-start.5
  50.7 9.4 %shard_map.96.refs_0_ = f32[64,16,128]{2,1,0:T(8,128)S(1)} custom-call(s32[32768]{0:T(1024)S(1)} %pad_add_fusion.1.refs_0_, s32[64]{0:T(128)S(1)} %get-tuple-element.49.refs_1_, f32[5056,128]{1,0:T(8,128)S(1)} %coefficient_rows.1.refs_6_.refs_2_, f32[4112,128]{1,0:T(8,128)S(1)} %get-tuple-element.35.refs_3_), custom_call_target="tpu_custom_call" | custom-call | flops 8589934592 | bytes 6291456 | tf_op jit(solution)/shard_map/pallas_call | solution.py:391
  60.1 4.1 %collective-permute-done.6.refs_2_ = bf16[24,16,128]{2,1,0:T(8,128)(2,1)S(1)} collective-permute-done((bf16[24,16,128]{2,1,0:T(8,128)(2,1)S(1)}, bf16[24,16,128]{2,1,0:T(8,128)(2,1)S(1)}, u32[]{:S(2)}, u32[]{:S(2)}) %collective-permute-start.6) | collective-permute-done | bytes 98336 | tf_op jit(solution)/shard_map/ppermute | solution.py:440
  64.3 4.1 %collective-permute-done.5.refs_1_ = bf16[40,16,128]{2,1,0:T(8,128)(2,1)S(1)} collective-permute-done((bf16[40,16,128]{2,1,0:T(8,128)(2,1)S(1)}, bf16[40,16,128]{2,1,0:T(8,128)(2,1)S(1)}, u32[]{:S(2)}, u32[]{:S(2)}) %collective-permute-start.5) | collective-permute-done | bytes 163872 | tf_op jit(solution)/shard_map/ppermute | solution.py:440
  68.4 0.9 %finish.1 = bf16[64,2016]{1,0:T(8,128)(2,1)} custom-call(f32[64,16,128]{2,1,0:T(8,128)S(1)} %shard_map.96.refs_0_, bf16[40,16,128]{2,1,0:T(8,128)(2,1)S(1)} %collective-permute-done.5.refs_1_, bf16[24,16,128]{2,1,0:T(8,128)(2,1)S(1)} %collective-permute-done.6.refs_2_), custom_call_target="tpu_custom_call" | custom-call | tf_op jit(solution)/shard_map/finish/pallas_call | solution.py:427
  (9 shorter events, 0.1 us)
Async XLA Ops:
  2.2 3.5 %collective-permute-start = (bf16[2,2019]{1,0:T(2,128)(2,1)S(1)}, bf16[2,2019]{1,0:T(2,128)(2,1)S(1)}, u32[]{:S(2)}, u32[]{:S(2)}) collective-permute-start(bf16[2,2019]{1,0:T(2,128)(2,1)S(1)} %get-tuple-element.21), channel_id=1, source_target_pairs={{1,0},{2,1},{3,2},{4,3},{5,4},{6,5},{7,6},{8,7},{9,8},{10,9},{11,1... | collective-permute-start | bytes 24236 | tf_op jit(solution)/shard_map/ppermute | solution.py:453
  5.7 3.3 %copy-start.1 = (s32[64,189]{1,0:T(8,128)S(1)}, s32[64,189]{1,0:T(8,128)}, u32[]{:S(2)}) copy-start(s32[64,189]{1,0:T(8,128)} %param.15) | copy-start | bytes 145156
  5.7 3.3 %copy-start.2 = (s32[64,189]{1,0:T(8,128)S(1)}, s32[64,189]{1,0:T(8,128)}, u32[]{:S(2)}) copy-start(s32[64,189]{1,0:T(8,128)} %param.14) | copy-start | bytes 145156
  9.1 12.5 %collective-permute-start.1 = (s32[64,189]{1,0:T(8,128)S(1)}, s32[64,189]{1,0:T(8,128)S(1)}, u32[]{:S(2)}, u32[]{:S(2)}) collective-permute-start(s32[64,189]{1,0:T(8,128)S(1)} %get-tuple-element.46), channel_id=1, source_target_pairs={{0,252},{1,253},{2,254},{3,255},{4,0},{5,1},{6,2},{7,3},{8,4},{9,5... | collective-permute-start | bytes 145160 | tf_op jit(solution)/shard_map/ppermute | solution.py:440
  19.7 9.4 %collective-permute-start.3 = (bf16[64,16,128]{2,1,0:T(8,128)(2,1)S(1)}, bf16[64,16,128]{2,1,0:T(8,128)(2,1)S(1)}, u32[]{:S(2)}, u32[]{:S(2)}) collective-permute-start(bf16[64,16,128]{2,1,0:T(8,128)(2,1)S(1)} %get-tuple-element.34.refs_5_), channel_id=1, source_target_pairs={{0,2},{1,3},{2,4},{3,5},{4,6},{5,7},{6,8},{7,9},{8,10},{9,11},{10,... | collective-permute-start | bytes 786440 | tf_op jit(solution)/shard_map/ppermute | solution.py:440
  19.7 20.2 %collective-permute-start.2 = (bf16[64,16,128]{2,1,0:T(8,128)(2,1)S(1)}, bf16[64,16,128]{2,1,0:T(8,128)(2,1)S(1)}, u32[]{:S(2)}, u32[]{:S(2)}) collective-permute-start(bf16[64,16,128]{2,1,0:T(8,128)(2,1)S(1)} %get-tuple-element.34.refs_5_), channel_id=1, source_target_pairs={{0,1},{1,4},{2,3},{3,6},{4,5},{5,8},{6,7},{7,10},{8,9},{9,12},{10,... | collective-permute-start | bytes 786440 | tf_op jit(solution)/shard_map/ppermute | solution.py:460
  25.1 4.0 %copy-start = (bf16[316,2016]{1,0:T(8,128)(2,1)S(1)}, bf16[316,2016]{1,0:T(8,128)(2,1)}, u32[]{:S(2)}) copy-start(bf16[316,2016]{1,0:T(8,128)(2,1)} %refs_0_.1) | copy-start | bytes 3822340
  29.1 10.8 %collective-permute-start.4 = (bf16[64,16,128]{2,1,0:T(8,128)(2,1)S(1)}, bf16[64,16,128]{2,1,0:T(8,128)(2,1)S(1)}, u32[]{:S(2)}, u32[]{:S(2)}) collective-permute-start(bf16[64,16,128]{2,1,0:T(8,128)(2,1)S(1)} %collective-permute-done.3.refs_3_), channel_id=1, source_target_pairs={{0,1},{1,0},{2,3},{3,2},{4,5},{5,4},{6,7},{7,6},{8,9},{9,8},{10,11... | collective-permute-start | bytes 786440 | tf_op jit(solution)/shard_map/ppermute | solution.py:461
  50.5 13.7 %collective-permute-start.6 = (bf16[24,16,128]{2,1,0:T(8,128)(2,1)S(1)}, bf16[24,16,128]{2,1,0:T(8,128)(2,1)S(1)}, u32[]{:S(2)}, u32[]{:S(2)}) collective-permute-start(bf16[24,16,128]{2,1,0:T(8,128)(2,1)S(1)} %shard_map.97), channel_id=1, source_target_pairs={{0,4},{1,5},{2,6},{3,7},{4,8},{5,9},{6,10},{7,11},{8,12},{9,13},{1... | collective-permute-start | bytes 294920 | tf_op jit(solution)/shard_map/ppermute | solution.py:440
  50.6 17.8 %collective-permute-start.5 = (bf16[40,16,128]{2,1,0:T(8,128)(2,1)S(1)}, bf16[40,16,128]{2,1,0:T(8,128)(2,1)S(1)}, u32[]{:S(2)}, u32[]{:S(2)}) collective-permute-start(bf16[40,16,128]{2,1,0:T(8,128)(2,1)S(1)} %get-tuple-element.36), channel_id=1, source_target_pairs={{0,4},{1,5},{2,6},{3,7},{4,8},{5,9},{6,10},{7,11},{8,12},{9,13},{1... | collective-permute-start | bytes 491528 | tf_op jit(solution)/shard_map/ppermute | solution.py:440
